TPU v7x, 512 devices: a whole 4x4x16 slice. The times are simulated.
512 devices in a mesh: dp: 128 (over z, y, core), mp: 4 (over x).
Axes of the slice: x: 4, y: 4, z: 16, core: 2. Of those that a mesh axis runs over, the one named last changes fastest.
Arguments:
- item_table: bfloat16 [262144, 256], P('dp'), may hold values from -6 to 6
- history_owner: int32 [32768, 1], P(('dp', 'mp')), may hold values from 0 to 127; in each aligned block of 64 rows (0 to 63, 64 to 127, ...) at most 4 rows name the same one
- history_row: int32 [32768], P(('dp', 'mp')), may hold values from 0 to 2047
- w_in: bfloat16 [256, 512], replicated, may hold values from -0.375 to 0.375
- conv_a: bfloat16 [4, 3, 512, 512], P(None, None, None, 'mp'), may hold values from -0.15625 to 0.15625
- conv_b: bfloat16 [4, 3, 512, 512], P(None, None, 'mp'), may hold values from -0.15625 to 0.15625
- gains: float32 [4, 512], replicated, may hold values from 0.5 to 1.5
- w_out: bfloat16 [512, 256], replicated, may hold values from -0.25 to 0.25
- cand_row: int32 [128, 128, 8], P('dp'), may hold values from 0 to 2047
- cand_count: int32 [128, 128], P('dp'), may hold values from 1 to 8, 512 in all within a row
- pos_owner: int32 [128], P('dp'), may hold values from 0 to 127
Outputs:
- scores: float32 [128, 128, 8], P('dp')
- user_loss: float32 [128], P('dp')
Inputs may be any that keep to these rules, and one draw needn't show every extreme that they name: `history_owner`: within each aligned block of 64 events no owner appears more than 4 times, and some owner appears exactly 4 times. `cand_count`: each user's counts sum to 512; the largest of them is 8.
All inputs are finite; a program needn't handle non-finite values.
Results may differ from a plain program's by a relative error of at most 0.025.
Values may be sent and summed in bfloat16 or wider, within the bound.
No kernel may reach another device: no remote copies, remote signals or barrier semaphores. Data moves between devices by JAX's collectives and lax.ppermute only.
A program may use at most 64 MiB of HBM per device.

v0:
```python
import jax
import jax.numpy as jnp
from jax import lax
from jax.sharding import PartitionSpec as P

C = 512
BLOCKS = 4
LEN = 256


def shift_rows(values, offset):
    padded = jnp.pad(values, ((0, 0), (offset, 0), (0, 0)))
    return padded[:, : values.shape[1], :]


def causal_taps(values, dilation):
    return jnp.concatenate(
        [values, shift_rows(values, dilation), shift_rows(values, 2 * dilation)], axis=-1
    )


def lookup(item_table, owner_ids, row_ids, fetch_len, capacity, dp_count):
    groups = owner_ids.shape[0] // fetch_len
    owner_grid = owner_ids.reshape(groups, fetch_len)
    onehot = (
        owner_grid[:, :, None] == jnp.arange(dp_count, dtype=jnp.int32)[None, None, :]
    ).astype(jnp.int32)
    before = jnp.cumsum(onehot, axis=1) - onehot
    slot_within = jnp.sum(before * onehot, axis=2)
    slot_ids = (slot_within + jnp.arange(groups, dtype=jnp.int32)[:, None] * capacity).reshape(-1)
    flat_owner = owner_grid.reshape(-1)
    requests = (
        jnp.zeros((groups * capacity, dp_count), jnp.int32).at[slot_ids, flat_owner].set(row_ids)
    )
    picked = item_table[lax.all_to_all(requests, "dp", split_axis=1, concat_axis=1, tiled=True)]
    arrived = lax.all_to_all(picked, "dp", split_axis=1, concat_axis=1, tiled=True)
    return arrived[slot_ids, flat_owner]


def per_device(
    item_table,
    history_owner,
    history_row,
    w_in,
    conv_a,
    conv_b,
    gains,
    w_out,
    cand_row,
    cand_count,
    pos_owner,
):
    dp_count = lax.axis_size("dp")
    mp_count = lax.axis_size("mp")
    fetch_len = history_row.shape[0]
    capacity = max(4, 2 * fetch_len // dp_count)
    owner_ids = history_owner[:, 0]
    embedded = lookup(item_table, owner_ids, history_row, fetch_len, capacity, dp_count)
    embedded = lax.all_gather(embedded, "mp", axis=0, tiled=True)
    user_count = cand_row.shape[0]
    hidden = jnp.dot(embedded, w_in, preferred_element_type=jnp.float32).astype(jnp.bfloat16)
    quarter = C // mp_count
    for block_idx in range(BLOCKS):
        dilation = 1 if block_idx % 2 == 0 else 4
        taps_a = causal_taps(hidden.reshape(user_count, LEN, C), dilation).reshape(-1, 3 * C)
        rectified = jax.nn.relu(
            jnp.dot(
                taps_a,
                conv_a[block_idx].reshape(3 * C, quarter),
                preferred_element_type=jnp.float32,
            )
        ).astype(jnp.bfloat16)
        taps_b = causal_taps(rectified.reshape(user_count, LEN, quarter), 2 * dilation).reshape(
            -1, 3 * quarter
        )
        partial_value = jnp.dot(
            taps_b, conv_b[block_idx].reshape(3 * quarter, C), preferred_element_type=jnp.float32
        )
        gain_row = gains[block_idx]
        branch = lax.psum(partial_value.astype(jnp.bfloat16), "mp").astype(jnp.float32)
        summed = hidden.astype(jnp.float32) + branch
        row_mean = jnp.mean(summed, axis=1, keepdims=True)
        row_msq = jnp.mean(summed * summed, axis=1, keepdims=True)
        row_var = row_msq - row_mean * row_mean
        hidden = ((summed - row_mean) * lax.rsqrt(row_var + 1e-05) * gain_row).astype(jnp.bfloat16)
    last_rows = hidden.reshape(user_count, LEN, C)[:, LEN - 1, :]
    user_vec = jnp.dot(last_rows, w_out, preferred_element_type=jnp.float32).astype(jnp.bfloat16)
    cand_rows = lax.all_to_all(
        item_table[lax.all_to_all(cand_row, "dp", split_axis=1, concat_axis=1, tiled=True)],
        "dp",
        split_axis=1,
        concat_axis=1,
        tiled=True,
    )
    raw_scores = 0.25 * jnp.einsum(
        "ue,unce->unc", user_vec, cand_rows, preferred_element_type=jnp.float32
    )
    valid_slot = (
        jnp.arange(raw_scores.shape[2], dtype=jnp.int32)[None, None, :] < cand_count[:, :, None]
    )
    scores = jnp.where(valid_slot, raw_scores, 0.0)
    exp_total = jnp.sum(jnp.where(valid_slot, jnp.exp(raw_scores), 0.0), axis=(1, 2))
    positive = jnp.take_along_axis(raw_scores[:, :, 0], pos_owner[:, None], axis=1)[:, 0]
    user_loss = jnp.log(exp_total) - positive
    return (scores, user_loss)


def solution(mesh):
    return jax.shard_map(
        per_device,
        mesh=mesh,
        in_specs=(
            P("dp", None),
            P(("dp", "mp"), None),
            P(("dp", "mp")),
            P(),
            P(None, None, None, "mp"),
            P(None, None, "mp", None),
            P(),
            P(),
            P("dp", None, None),
            P("dp", None),
            P("dp"),
        ),
        out_specs=(P("dp", None, None), P("dp")),
        check_vma=False,
    )
```

profile of v0, /device:TPU:24, one launch (start us, length us, event | category | flops | bytes accessed | tf_op | source)
XLA Modules:
  0.0 345.8 jit_solution(17920219697878644076)
XLA Ops:
  7.2 0.0 copy-start
  7.2 0.8 fusion.48
  8.0 0.1 reduce_window_sum.11
  8.1 0.8 select_reduce_fusion
  8.9 0.7 fusion.52
  9.6 5.7 %scatter_fusion = s32[4,128]{1,0:T(4,128)S(1)} fusion(s32[4,128]{1,0:T(4,128)S(1)} %broadcast.205, s32[64]{0:T(128)S(1)} %get-tuple-element.21, s32[64]{0:T(128)} %param.13), kind=kCustom, calls=%fused_computation.3 | custom fusion | bytes 1280 | tf_op jit(solution)/shard_map/scatter | solution.py:33
  15.4 0.1 copy.19
  15.5 32.8 %all_to_all.24 = s32[4,128,1]{0,2,1:T(1,128)S(1)} all-to-all(s32[4,128,1]{0,2,1:T(1,128)S(1)} %copy.19), channel_id=1, replica_groups=mesh['dp'=128,'mp'=4] {'dp'}, dimensions={1} | all-to-all | bytes 4096 | tf_op jit(solution)/shard_map/all_to_all | solution.py:35
  48.3 0.1 compare_select_fusion.1
  48.4 0.1 copy.20
  48.4 0.0 copy-done
  48.5 2.0 gather_fusion
  50.4 0.9 copy.21
  51.3 6.9 %all-to-all-start.1 = ((bf16[4,128,256]{2,0,1:T(4,128)(2,1)}), bf16[4,128,256]{2,0,1:T(4,128)(2,1)S(1)}, u32[]{:S(2)}, u32[]{:S(2)}) async-start(bf16[4,128,256]{2,0,1:T(4,128)(2,1)} %copy.21), calls=%async_computation.1 | async-start | bytes 524288 | tf_op jit(solution)/shard_map/all_to_all | solution.py:36
  58.3 0.0 all-reduce.21.cloned.1.call-start
  58.3 1.1 fusion.62
  59.4 0.8 copy-done.2
  60.1 1.0 fusion.63
  61.1 18.9 %all-to-all-done.1 = bf16[4,128,256]{2,0,1:T(4,128)(2,1)S(1)} async-done(((bf16[4,128,256]{2,0,1:T(4,128)(2,1)}), bf16[4,128,256]{2,0,1:T(4,128)(2,1)S(1)}, u32[]{:S(2)}, u32[]{:S(2)}) %all-to-all-start.1) | async-done | bytes 262176 | tf_op jit(solution)/shard_map/all_to_all | solution.py:36
  80.1 0.8 gather_fusion.1
  80.9 12.3 %all_gather.3 = bf16[256,256]{1,0:T(8,128)(2,1)S(1)} all-gather(bf16[64,256]{1,0:T(8,128)(2,1)S(1)} %gather_fusion.1), channel_id=1, replica_groups=mesh['dp'=128,'mp'=4] {'mp'}, dimensions={0}, use_global_device_ids=true | all-gather | bytes 163840 | tf_op jit(solution)/shard_map/all_gather | solution.py:59
  93.2 0.2 convolution_convert_fusion.4
  93.5 0.1 pad_slice_fusion.7
  93.6 1.4 fusion.7
  95.1 1.0 convolution_convert_fusion.3
  96.1 0.0 all-reduce.21.cloned.1.call-update
  96.1 0.0 all-reduce.23.cloned.1.call-start
  96.2 48.8 %all-reduce.21.cloned.1.call-done = bf16[256,512]{1,0:T(8,128)(2,1)} async-done(((bf16[256,512]{1,0:T(8,128)(2,1)}), bf16[256,512]{1,0:T(8,128)(2,1)}) %all-reduce.21.cloned.1.call-update) | async-done | bytes 262160 | tf_op jit(solution)/shard_map/psum | solution.py:80
  145.0 1.1 fusion.26
  146.2 1.1 multiply_convert_fusion.3
  147.3 0.1 pad_slice_fusion.5
  147.4 0.4 fusion.6
  147.8 1.0 convolution_convert_fusion.2
  148.8 0.0 all-reduce.23.cloned.1.call-update
  148.8 0.7 copy.23
  149.5 16.5 %all-to-all-start.2 = ((s32[1,128,8]{2,0,1:T(1,128)}), s32[1,128,8]{2,0,1:T(1,128)S(1)}, u32[]{:S(2)}, u32[]{:S(2)}) async-start(s32[1,128,8]{2,0,1:T(1,128)} %copy.23), calls=%async_computation.2 | async-start | bytes 131072 | tf_op jit(solution)/shard_map/all_to_all | solution.py:89
  166.0 0.0 all-reduce.25.cloned.1.call-start
  166.1 40.7 %all-reduce.23.cloned.1.call-done = bf16[256,512]{1,0:T(8,128)(2,1)} async-done(((bf16[256,512]{1,0:T(8,128)(2,1)}), bf16[256,512]{1,0:T(8,128)(2,1)}) %all-reduce.23.cloned.1.call-update) | async-done | bytes 262160 | tf_op jit(solution)/shard_map/psum | solution.py:80
  206.7 1.1 fusion.27
  207.9 1.1 multiply_convert_fusion.2
  209.0 0.1 pad_slice_fusion.3
  209.1 1.4 fusion.5
  210.6 1.0 convolution_convert_fusion.1
  211.6 0.0 all-reduce.25.cloned.1.call-update
  211.6 0.2 fusion.47
  211.8 0.1 reshape.320
  211.9 5.0 %gather_fusion.2 = bf16[1024,256]{1,0:T(8,128)(2,1)} fusion(bf16[2048,256]{1,0:T(8,128)(2,1)S(1)} %copy-done, s32[1024]{0:T(1024)S(1)} %broadcast_clamp_fusion), kind=kCustom, calls=%fused_computation.2 | custom fusion | bytes 1052672 | tf_op jit(solution)/shard_map/gather | solution.py:89
  216.9 16.5 %all-to-all-start.3 = ((bf16[1,128,8,256]{3,2,0,1:T(8,128)(2,1)}), bf16[1,128,8,256]{3,2,0,1:T(8,128)(2,1)S(1)}, u32[]{:S(2)}, u32[]{:S(2)}) async-start(bf16[1,128,8,256]{3,2,0,1:T(8,128)(2,1)} %bitcast.39), calls=%async_computation.3 | async-start | bytes 1048576 | tf_op jit(solution)/shard_map/all_to_all | solution.py:88
  233.4 0.0 all-reduce.27.cloned.1.call-start
  233.4 36.1 %all-reduce.25.cloned.1.call-done = bf16[256,512]{1,0:T(8,128)(2,1)} async-done(((bf16[256,512]{1,0:T(8,128)(2,1)}), bf16[256,512]{1,0:T(8,128)(2,1)}) %all-reduce.25.cloned.1.call-update) | async-done | bytes 262160 | tf_op jit(solution)/shard_map/psum | solution.py:80
  269.6 1.1 fusion.28
  270.7 1.1 multiply_convert_fusion.1
  271.8 0.1 pad_slice_fusion.1
  271.9 0.4 fusion.4
  272.3 1.0 convolution_convert_fusion
  273.3 0.0 all-reduce.27.cloned.1.call-update
  274.0 57.3 %all-reduce.27.cloned.1.call-done = bf16[256,512]{1,0:T(8,128)(2,1)} async-done(((bf16[256,512]{1,0:T(8,128)(2,1)}), bf16[256,512]{1,0:T(8,128)(2,1)}) %all-reduce.27.cloned.1.call-update) | async-done | bytes 262160 | tf_op jit(solution)/shard_map/psum | solution.py:80
  331.3 1.1 fusion.29
  332.4 1.1 fusion.30
  333.6 0.1 fusion.50
  333.7 1.2 fusion.24
  335.0 0.1 copy.25
  335.0 1.2 select_reduce_fusion.1
  337.0 0.6 constant_dynamic-slice_fusion
  (37 shorter events, 0.3 us)
Async XLA Ops:
  7.2 41.3 %copy-start = (bf16[2048,256]{1,0:T(8,128)(2,1)S(1)}, bf16[2048,256]{1,0:T(8,128)(2,1)}, u32[]{:S(2)}) copy-start(bf16[2048,256]{1,0:T(8,128)(2,1)} %param.11) | copy-start | bytes 3145732
  48.5 9.8 %copy-start.1 = (bf16[4,3,512,128]{3,2,1,0:T(8,128)(2,1)S(1)}, bf16[4,3,512,128]{3,2,1,0:T(8,128)(2,1)}, u32[]{:S(2)}) copy-start(bf16[4,3,512,128]{3,2,1,0:T(8,128)(2,1)} %param.15) | copy-start | bytes 4718596
  51.3 28.7 %all-to-all-start.1 = ((bf16[4,128,256]{2,0,1:T(4,128)(2,1)}), bf16[4,128,256]{2,0,1:T(4,128)(2,1)S(1)}, u32[]{:S(2)}, u32[]{:S(2)}) async-start(bf16[4,128,256]{2,0,1:T(4,128)(2,1)} %copy.21), calls=%async_computation.1 | async-start | bytes 524288 | tf_op jit(solution)/shard_map/all_to_all | solution.py:36
  58.3 86.8 %all-reduce.21.cloned.1.call-start = ((), (), s32[]{:S(2)}) async-start(), calls=%async_computation.4 | async-start | bytes 524288 | tf_op jit(solution)/shard_map/psum | solution.py:80
  58.3 1.8 copy-start.2
  60.1 33.1 %copy-start.6 = (bf16[256,512]{1,0:T(8,128)(2,1)S(1)}, bf16[256,512]{1,0:T(8,128)(2,1)}, u32[]{:S(2)}) copy-start(bf16[256,512]{1,0:T(8,128)(2,1)} %param.14) | copy-start | bytes 786436
  93.6 1.5 copy-start.5
  93.6 2.6 copy-start.8
  95.1 52.3 %copy-start.4 = (bf16[1,3,512,128]{3,2,1,0:T(8,128)(2,1)S(1)}, bf16[1,3,512,128]{3,2,1,0:T(8,128)(2,1)}, u32[]{:S(2)}) copy-start(bf16[1,3,512,128]{3,2,1,0:T(8,128)(2,1)} %get-tuple-element.24) | copy-start | bytes 1179652
  96.1 110.6 %all-reduce.23.cloned.1.call-start = ((), (), s32[]{:S(2)}) async-start(), calls=%async_computation.5 | async-start | bytes 524288 | tf_op jit(solution)/shard_map/psum | solution.py:80
  147.4 1.4 copy-start.9
  149.5 62.1 %all-to-all-start.2 = ((s32[1,128,8]{2,0,1:T(1,128)}), s32[1,128,8]{2,0,1:T(1,128)S(1)}, u32[]{:S(2)}, u32[]{:S(2)}) async-start(s32[1,128,8]{2,0,1:T(1,128)} %copy.23), calls=%async_computation.2 | async-start | bytes 131072 | tf_op jit(solution)/shard_map/all_to_all | solution.py:89
  166.0 103.6 %all-reduce.25.cloned.1.call-start = ((), (), s32[]{:S(2)}) async-start(), calls=%async_computation.6 | async-start | bytes 524288 | tf_op jit(solution)/shard_map/psum | solution.py:80
  209.1 1.5 copy-start.3
  216.9 116.8 %all-to-all-start.3 = ((bf16[1,128,8,256]{3,2,0,1:T(8,128)(2,1)}), bf16[1,128,8,256]{3,2,0,1:T(8,128)(2,1)S(1)}, u32[]{:S(2)}, u32[]{:S(2)}) async-start(bf16[1,128,8,256]{3,2,0,1:T(8,128)(2,1)} %bitcast.39), calls=%async_computation.3 | async-start | bytes 1048576 | tf_op jit(solution)/shard_map/all_to_all | solution.py:88
  233.4 97.9 %all-reduce.27.cloned.1.call-start = ((), (), s32[]{:S(2)}) async-start(), calls=%async_computation.7 | async-start | bytes 524288 | tf_op jit(solution)/shard_map/psum | solution.py:80
  272.3 61.3 %copy-start.7 = (bf16[512,256]{1,0:T(8,128)(2,1)S(1)}, bf16[512,256]{1,0:T(8,128)(2,1)}, u32[]{:S(2)}) copy-start(bf16[512,256]{1,0:T(8,128)(2,1)} %param.18) | copy-start | bytes 786436
  272.3 62.7 %copy-start.10 = (s32[1,128]{1,0:T(1,128)S(1)}, s32[1,128]{1,0:T(1,128)}, u32[]{:S(2)}) copy-start(s32[1,128]{1,0:T(1,128)} %param.20) | copy-start | bytes 1540
Sparse Core Ops, SparseCore 0:
  96.2 48.7 all-reduce.20
  148.9 57.7 all-reduce.22
  211.7 57.7 all-reduce.24
  273.5 57.7 all-reduce.26
where the time goes:
time: 347 us; the launch traced here: 346 us
  waiting for transfers between devices  202 us (58%)
  blocking collectives  45.2 us (13%)
  starting transfers between devices  40 us (12%)
  local copies, waits for them, and re-layouts  19.4 us (6%)
  between operations  17.2 us (5%)
  other arithmetic  12.9 us (4%)
  matrix products  9.15 us (3%)
    psum x4, waiting for transfers between devices, per_device(): lax.psum(partial_value.astype(jnp.bfloat16), 'mp').astype(jnp.float32)  183 us
    all_to_all x1, blocking collectives, lookup(): lax.all_to_all(requests, 'dp', split_axis=1, concat_axis=1, tiled=True)  32.8 us
    all_to_all x1, waiting for transfers between devices, lookup(): lax.all_to_all(picked, 'dp', split_axis=1, concat_axis=1, tiled=True)  18.9 us
    all_to_all x1, starting transfers between devices, per_device(): lax.all_to_all(cand_row, 'dp', split_axis=1, concat_axis=1, tiled=True)  16.5 us
    all_to_all x1, starting transfers between devices, per_device(): lax.all_to_all(item_table[lax.all_to_all(cand_row, 'dp', split_axis=1, co...  16.5 us
    all_gather x1, blocking collectives, per_device(): embedded = lax.all_gather(embedded, 'mp', axis=0, tiled=True)  12.3 us
  transfers between devices with their start and end apart: 7, of which 5 were waited for; matrix products, arithmetic and copies ran while one was open for 5% of the time, Pallas kernels for 0%

commit v1 on v0

v1 whole, which is shorter than its diff:
```python
import jax
import jax.numpy as jnp
from jax import lax
from jax.sharding import PartitionSpec as P

C = 512
BLOCKS = 4
LEN = 256
CAP = 4
CPO = 8
REACH = 61
WINDOW = 64
READ_FROM = (0, 32, 32, 56)

F32 = jnp.float32
BF16 = jnp.bfloat16


def exchange(values, axis):
    return lax.all_to_all(values, axis, split_axis=0, concat_axis=0, tiled=True)


def share(values, axis_size):
    return exchange(jnp.broadcast_to(values[None], (axis_size,) + values.shape), "mp")


def shifted_sum(parts, gap):
    total = parts[0]
    for k in (1, 2):
        total = total + jnp.pad(parts[k], ((k * gap, 0), (0, 0)))[: parts[k].shape[0]]
    return total


def pick_rows(table, ids):
    onehot = (ids[:, None] == jnp.arange(table.shape[0], dtype=jnp.int32)[None, :]).astype(BF16)
    return jnp.dot(onehot, table, preferred_element_type=F32).astype(BF16)


def per_device(
    item_table,
    history_owner,
    history_row,
    w_in,
    conv_a,
    conv_b,
    gains,
    w_out,
    cand_row,
    cand_count,
    pos_owner,
):
    dp_count = lax.axis_size("dp")
    mp_count = lax.axis_size("mp")
    mp_index = lax.axis_index("mp")
    last = mp_count - 1
    owner_ids = history_owner[:, 0]
    event = jnp.arange(WINDOW, dtype=jnp.int32)
    same = owner_ids[:, None] == owner_ids[None, :]
    slot = jnp.sum((same & (event[None, :] < event[:, None])).astype(jnp.int32), axis=1)
    of_owner = owner_ids[None, :] == jnp.arange(dp_count, dtype=jnp.int32)[:, None]
    slots = jnp.arange(CAP, dtype=jnp.int32)
    placed = of_owner[:, None, :] & (slot[None, :] == slots[:, None])[None]
    history_asks = jnp.sum(jnp.where(placed, history_row[None, None, :], 0), axis=2)
    cand_padded = jnp.pad(cand_row[0], ((0, 0), (0, 3 * last + CAP - CPO)))
    cand_asks = lax.dynamic_slice(
        cand_padded, (0, 3 * jnp.minimum(mp_index, last - 1)), (dp_count, CAP)
    )
    asks = jnp.where(mp_index == last, history_asks, cand_asks)
    asked = exchange(jnp.pad(asks, ((0, 0), (0, 16 - CAP))), "dp")[:, :CAP]
    picked = pick_rows(item_table, asked.reshape(-1)).reshape(dp_count, CAP, -1)
    arrived = exchange(picked, "dp")
    embedded = pick_rows(arrived.reshape(dp_count * CAP, -1), owner_ids * CAP + slot)
    embedded = share(embedded, mp_count)[last]
    hidden = jnp.dot(embedded, w_in, preferred_element_type=F32).astype(BF16)
    cand_all = share(arrived, mp_count)
    cand_rows = jnp.concatenate(
        [cand_all[0][:, :3], cand_all[1][:, :3], cand_all[2][:, : CPO - 6]], axis=1
    )
    for block_idx in range(BLOCKS):
        gap = 1 if block_idx % 2 == 0 else 4
        rectified = jax.nn.relu(
            shifted_sum(
                [jnp.dot(hidden, conv_a[block_idx, k], preferred_element_type=F32) for k in range(3)],
                gap,
            )
        ).astype(BF16)
        partial_value = shifted_sum(
            [jnp.dot(rectified, conv_b[block_idx, k], preferred_element_type=F32) for k in range(3)],
            2 * gap,
        ).astype(BF16)
        keep = READ_FROM[block_idx] - (WINDOW - hidden.shape[0])
        parts = share(partial_value[keep:], mp_count).astype(F32)
        summed = hidden[keep:].astype(F32) + (parts[0] + parts[1] + parts[2] + parts[3])
        row_mean = jnp.mean(summed, axis=1, keepdims=True)
        row_msq = jnp.mean(summed * summed, axis=1, keepdims=True)
        row_var = row_msq - row_mean * row_mean
        hidden = ((summed - row_mean) * lax.rsqrt(row_var + 1e-05) * gains[block_idx]).astype(BF16)
    user_vec = jnp.dot(hidden[-1:], w_out, preferred_element_type=F32).astype(BF16)
    raw_scores = 0.25 * jnp.einsum(
        "ue,nce->unc", user_vec, cand_rows, preferred_element_type=F32
    )
    valid_slot = jnp.arange(CPO, dtype=jnp.int32)[None, None, :] < cand_count[:, :, None]
    scores = jnp.where(valid_slot, raw_scores, 0.0)
    exp_total = jnp.sum(jnp.where(valid_slot, jnp.exp(raw_scores), 0.0), axis=(1, 2))
    is_positive = jnp.arange(dp_count, dtype=jnp.int32)[None, :] == pos_owner[:, None]
    positive = jnp.sum(jnp.where(is_positive, raw_scores[:, :, 0], 0.0), axis=1)
    user_loss = jnp.log(exp_total) - positive
    return (scores, user_loss)


def solution(mesh):
    return jax.shard_map(
        per_device,
        mesh=mesh,
        in_specs=(
            P("dp", None),
            P(("dp", "mp"), None),
            P(("dp", "mp")),
            P(),
            P(None, None, None, "mp"),
            P(None, None, "mp", None),
            P(),
            P(),
            P("dp", None, None),
            P("dp", None),
            P("dp"),
        ),
        out_specs=(P("dp", None, None), P("dp")),
        check_vma=False,
    )
```

time: 347 us -> 144 us (0.41)
  waiting for transfers between devices: 202 us -> 35.8 us
  starting transfers between devices: 40 us -> 13.8 us
  blocking collectives: 45.2 us -> 67.4 us
  local copies, waits for them, and re-layouts: 19.4 us -> 5.36 us
  between operations: 17.2 us -> 4.15 us
  other arithmetic: 12.9 us -> 6.03 us
    psum x4 -> x0, waiting for transfers between devices: 183 us -> none  [per_device(): lax.psum(partial_value.astype(jnp.bfloat16), 'mp').astype(jnp.float32)]
    all_to_all x1 -> x5, blocking collectives: 32.8 us -> 67.4 us  [exchange(): return lax.all_to_all(values, axis, split_axis=0, concat_axis=0, tiled=True)]
    all_to_all x3, starting transfers between devices: 39.8 us -> 13.8 us  [exchange(): return lax.all_to_all(values, axis, split_axis=0, concat_axis=0, tiled=True)]
    all_to_all x3, waiting for transfers between devices: 18.9 us -> 35.8 us  [exchange(): return lax.all_to_all(values, axis, split_axis=0, concat_axis=0, tiled=True)]
    all_gather x1 -> x0, blocking collectives: 12.3 us -> none  [per_device(): embedded = lax.all_gather(embedded, 'mp', axis=0, tiled=True)]
    gather x5 -> x0, local copies, waits for them, and re-layouts: 9.25 us -> none  [the longest x1 4.96 us: per_device(): item_table[lax.all_to_all(cand_row, 'dp', split_axis=1, concat_axis=1, ti...]
    scatter x1 -> x0, local copies, waits for them, and re-layouts: 5.74 us -> none  [lookup(): jnp.zeros((groups * capacity, dp_count), jnp.int32).at[slot_ids, flat_owner]]
    reduce_sum x4, other arithmetic: 4.56 us -> 0.61 us  [per_device(): row_mean = jnp.mean(summed, axis=1, keepdims=True)]
  transfers between devices with their start and end apart: 7 -> 3, of which waited for: 5 -> 3; matrix products, arithmetic and copies ran while one was open for 5% -> 2% of each run, Pallas kernels for 0% -> 0%
where the time goes in v1:
time: 144 us; the launch traced here: 143 us
  blocking collectives  67.4 us (47%)
  waiting for transfers between devices  35.8 us (25%)
  starting transfers between devices  13.8 us (10%)
  matrix products  10.1 us (7%)
  other arithmetic  6.03 us (4%)
  local copies, waits for them, and re-layouts  5.36 us (4%)
  between operations  4.15 us (3%)
    all_to_all x5, blocking collectives, exchange(): return lax.all_to_all(values, axis, split_axis=0, concat_axis=0, tiled=True)  67.4 us
    all_to_all x3, waiting for transfers between devices, exchange(): return lax.all_to_all(values, axis, split_axis=0, concat_axis=0, tiled=True)  35.8 us
    all_to_all x3, starting transfers between devices, exchange(): return lax.all_to_all(values, axis, split_axis=0, concat_axis=0, tiled=True)  13.8 us
    dot_general x12, matrix products, per_device(): jnp.dot(rectified, conv_b[block_idx, k], preferred_element_type=F32)  4.39 us
  transfers between devices with their start and end apart: 3, of which 3 were waited for; matrix products, arithmetic and copies ran while one was open for 2% of the time, Pallas kernels for 0%

profile of v1, /device:TPU:24, one launch (start us, length us, event | category | flops | bytes accessed | tf_op | source)
XLA Modules:
  0.0 142.7 jit_solution(12837030724967694497)
XLA Ops:
  0.6 0.9 convert_reduce_fusion
  1.6 0.7 iota_compare_fusion.6
  2.4 0.8 select_reduce_fusion
  3.1 0.7 fusion.104
  3.8 0.1 copy.15
  3.9 32.8 %all_to_all.47 = s32[128,1,16]{2,1,0:T(1,128)S(1)} all-to-all(s32[128,1,16]{2,1,0:T(1,128)S(1)} %copy.15), channel_id=1, replica_groups=mesh['dp'=128,'mp'=4] {'dp'}, dimensions={0} | all-to-all | bytes 16384 | tf_op jit(solution)/shard_map/all_to_all | solution.py:20
  36.8 0.1 eq.115
  36.9 0.9 fusion.2
  37.8 0.8 reshape.190
  38.5 6.9 %all-to-all-start.1 = ((bf16[128,4,256]{2,1,0:T(4,128)(2,1)}), bf16[128,4,256]{2,1,0:T(4,128)(2,1)S(1)}, u32[]{:S(2)}, u32[]{:S(2)}) async-start(bf16[128,4,256]{2,1,0:T(4,128)(2,1)} %reshape.190), calls=%async_computation.1 | async-start | bytes 524288 | tf_op jit(solution)/shard_map/all_to_all | solution.py:20
  45.5 21.8 %all-to-all-done.1 = bf16[128,4,256]{2,1,0:T(4,128)(2,1)S(1)} async-done(((bf16[128,4,256]{2,1,0:T(4,128)(2,1)}), bf16[128,4,256]{2,1,0:T(4,128)(2,1)S(1)}, u32[]{:S(2)}, u32[]{:S(2)}) %all-to-all-start.1) | async-done | bytes 262176 | tf_op jit(solution)/shard_map/all_to_all | solution.py:20
  67.2 0.1 reshape.191
  67.3 0.2 convolution_convert_fusion.1
  67.5 10.1 %all_to_all.48 = bf16[4,64,256]{2,1,0:T(8,128)(2,1)S(1)} all-to-all(bf16[4,64,256]{2,1,0:T(8,128)(2,1)S(1)} %broadcast_in_dim.33), channel_id=1, replica_groups=mesh['dp'=128,'mp'=4] {'mp'}, dimensions={0} | all-to-all | bytes 262144 | tf_op jit(solution)/shard_map/all_to_all | solution.py:20
  77.6 0.2 convolution_convert_fusion
  77.8 0.2 fusion.64
  78.0 0.2 fusion.66
  78.1 0.2 fusion.11
  78.3 1.0 fusion.59
  79.3 1.0 fusion.61
  80.4 1.1 fusion.4
  81.5 0.7 broadcast_in_dim.34
  82.2 3.4 %all-to-all-start.3 = ((bf16[4,64,512]{2,1,0:T(8,128)(2,1)}), bf16[4,64,512]{2,1,0:T(8,128)(2,1)S(1)}, u32[]{:S(2)}, u32[]{:S(2)}) async-start(bf16[4,64,512]{2,1,0:T(8,128)(2,1)} %broadcast_in_dim.34), calls=%async_computation.3 | async-start | bytes 524288 | tf_op jit(solution)/shard_map/all_to_all | solution.py:20
  85.6 6.6 %all-to-all-done.3 = bf16[4,64,512]{2,1,0:T(8,128)(2,1)S(1)} async-done(((bf16[4,64,512]{2,1,0:T(8,128)(2,1)}), bf16[4,64,512]{2,1,0:T(8,128)(2,1)S(1)}, u32[]{:S(2)}, u32[]{:S(2)}) %all-to-all-start.3) | async-done | bytes 262176 | tf_op jit(solution)/shard_map/all_to_all | solution.py:20
  92.3 0.1 fusion.117
  92.4 0.1 multiply_convert_fusion
  92.5 0.2 fusion.54
  92.7 0.2 fusion.56
  92.9 0.2 fusion.12
  93.0 0.6 copy-done.2
  93.6 0.1 fusion.48
  93.8 0.1 fusion.50
  93.9 0.1 fusion.52
  94.2 8.4 %all_to_all.49 = bf16[4,32,512]{2,1,0:T(8,128)(2,1)S(1)} all-to-all(bf16[4,32,512]{2,1,0:T(8,128)(2,1)S(1)} %broadcast_in_dim.35), channel_id=1, replica_groups=mesh['dp'=128,'mp'=4] {'mp'}, dimensions={0} | all-to-all | bytes 262144 | tf_op jit(solution)/shard_map/all_to_all | solution.py:20
  102.5 0.1 fusion.119
  102.7 0.1 multiply_convert_fusion.2
  102.8 0.1 fusion.43
  102.9 0.1 fusion.45
  103.0 0.1 fusion.17
  103.2 0.1 fusion.38
  103.3 0.1 fusion.40
  103.5 0.2 fusion.6
  103.6 8.4 %all_to_all.50 = bf16[4,32,512]{2,1,0:T(8,128)(2,1)S(1)} all-to-all(bf16[4,32,512]{2,1,0:T(8,128)(2,1)S(1)} %broadcast_in_dim.36), channel_id=1, replica_groups=mesh['dp'=128,'mp'=4] {'mp'}, dimensions={0} | all-to-all | bytes 262144 | tf_op jit(solution)/shard_map/all_to_all | solution.py:20
  112.0 0.2 fusion.118
  112.2 0.1 multiply_convert_fusion.1
  112.3 0.1 fusion.33
  112.5 0.1 fusion.35
  112.6 0.1 fusion.18
  112.8 0.1 fusion.27
  112.9 0.1 fusion.29
  113.0 0.1 fusion.31
  113.2 7.8 %all_to_all.51 = bf16[4,8,512]{2,1,0:T(8,128)(2,1)S(1)} all-to-all(bf16[4,8,512]{2,1,0:T(8,128)(2,1)S(1)} %broadcast_in_dim.37), channel_id=1, replica_groups=mesh['dp'=128,'mp'=4] {'mp'}, dimensions={0} | all-to-all | bytes 65536 | tf_op jit(solution)/shard_map/all_to_all | solution.py:20
  121.0 1.3 broadcast_in_dim.38
  122.3 3.5 %all-to-all-start.7 = ((bf16[4,128,4,256]{3,2,1,0:T(4,128)(2,1)}), bf16[4,128,4,256]{3,2,1,0:T(4,128)(2,1)S(1)}, u32[]{:S(2)}, u32[]{:S(2)}) async-start(bf16[4,128,4,256]{3,2,1,0:T(4,128)(2,1)} %broadcast_in_dim.38), calls=%async_computation.7 | async-start | bytes 2097152 | tf_op jit(solution)/shard_map/all_to_all | solution.py:20
  126.5 0.2 fusion.120
  126.6 0.6 slice.323
  127.2 0.6 slice.324
  127.8 1.4 %fusion.109 = f32[1,256]{1,0:T(1,128)S(1)} fusion(bf16[512,256]{1,0:T(8,128)(2,1)S(1)} %copy-done.4, f32[8,512]{1,0:T(8,128)S(1)} %get-tuple-element.10, f32[512]{0:T(512)S(1)} %bitcast.175, f32[1]{0:T(128)} %slice.324, f32[1]{0:T(128)} %slice.323), kind=kOutput, calls=%fused_computation.173 | convolution fusion | flops 264192 | bytes 267272 | tf_op jit(solution)/shard_map/dot_general | solution.py:98
  129.3 7.4 %all-to-all-done.7 = bf16[4,128,4,256]{3,2,1,0:T(4,128)(2,1)S(1)} async-done(((bf16[4,128,4,256]{3,2,1,0:T(4,128)(2,1)}), bf16[4,128,4,256]{3,2,1,0:T(4,128)(2,1)S(1)}, u32[]{:S(2)}, u32[]{:S(2)}) %all-to-all-start.7) | async-done | bytes 1048608 | tf_op jit(solution)/shard_map/all_to_all | solution.py:20
  136.7 0.3 slice_bitcast_fusion.2
  136.9 0.1 slice.330
  137.0 1.3 fusion.19
  138.4 1.2 select_reduce_fusion.1
  140.3 0.6 fusion.114
  (39 shorter events, 0.4 us)
Async XLA Ops:
  0.6 36.2 %copy-start = (bf16[2048,256]{1,0:T(8,128)(2,1)S(1)}, bf16[2048,256]{1,0:T(8,128)(2,1)}, u32[]{:S(2)}) copy-start(bf16[2048,256]{1,0:T(8,128)(2,1)} %param.11) | copy-start | bytes 3145732
  36.9 8.6 %copy-start.6 = (s32[64,1]{0,1:T(1,128)S(1)}, s32[64,1]{0,1:T(1,128)}, u32[]{:S(2)}) copy-start(s32[64,1]{0,1:T(1,128)} %param.12) | copy-start | bytes 772
  37.8 39.9 %copy-start.3 = (bf16[256,512]{1,0:T(8,128)(2,1)S(1)}, bf16[256,512]{1,0:T(8,128)(2,1)}, u32[]{:S(2)}) copy-start(bf16[256,512]{1,0:T(8,128)(2,1)} %param.14) | copy-start | bytes 786436
  37.8 40.0 %copy-start.1 = (bf16[4,3,512,128]{3,2,1,0:T(8,128)(2,1)S(1)}, bf16[4,3,512,128]{3,2,1,0:T(8,128)(2,1)}, u32[]{:S(2)}) copy-start(bf16[4,3,512,128]{3,2,1,0:T(8,128)(2,1)} %param.15) | copy-start | bytes 4718596
  38.5 28.7 %all-to-all-start.1 = ((bf16[128,4,256]{2,1,0:T(4,128)(2,1)}), bf16[128,4,256]{2,1,0:T(4,128)(2,1)S(1)}, u32[]{:S(2)}, u32[]{:S(2)}) async-start(bf16[128,4,256]{2,1,0:T(4,128)(2,1)} %reshape.190), calls=%async_computation.1 | async-start | bytes 524288 | tf_op jit(solution)/shard_map/all_to_all | solution.py:20
  67.5 18.0 %copy-start.5 = (f32[4,512]{1,0:T(4,128)S(1)}, f32[4,512]{1,0:T(4,128)}, u32[]{:S(2)}) copy-start(f32[4,512]{1,0:T(4,128)} %param.17) | copy-start | bytes 24580
  82.2 10.1 %all-to-all-start.3 = ((bf16[4,64,512]{2,1,0:T(8,128)(2,1)}), bf16[4,64,512]{2,1,0:T(8,128)(2,1)S(1)}, u32[]{:S(2)}, u32[]{:S(2)}) async-start(bf16[4,64,512]{2,1,0:T(8,128)(2,1)} %broadcast_in_dim.34), calls=%async_computation.3 | async-start | bytes 524288 | tf_op jit(solution)/shard_map/all_to_all | solution.py:20
  92.2 1.4 copy-start.2
  121.0 6.8 %copy-start.4 = (bf16[512,256]{1,0:T(8,128)(2,1)S(1)}, bf16[512,256]{1,0:T(8,128)(2,1)}, u32[]{:S(2)}) copy-start(bf16[512,256]{1,0:T(8,128)(2,1)} %param.18) | copy-start | bytes 786436
  122.3 14.4 %all-to-all-start.7 = ((bf16[4,128,4,256]{3,2,1,0:T(4,128)(2,1)}), bf16[4,128,4,256]{3,2,1,0:T(4,128)(2,1)S(1)}, u32[]{:S(2)}, u32[]{:S(2)}) async-start(bf16[4,128,4,256]{3,2,1,0:T(4,128)(2,1)} %broadcast_in_dim.38), calls=%async_computation.7 | async-start | bytes 2097152 | tf_op jit(solution)/shard_map/all_to_all | solution.py:20
  129.3 9.1 %copy-start.7 = (s32[1,128]{1,0:T(1,128)S(1)}, s32[1,128]{1,0:T(1,128)}, u32[]{:S(2)}) copy-start(s32[1,128]{1,0:T(1,128)} %param.20) | copy-start | bytes 1540

commit v2 on v1

v2 whole, which is shorter than its diff:
```python
import jax
import jax.numpy as jnp
from jax import lax
from jax.experimental import pallas as pl
from jax.experimental.pallas import tpu as pltpu
from jax.sharding import PartitionSpec as P


C = 512
QUARTER = 128
CAP = 4
CPO = 8
WINDOW = 64
LATE = 32
FIRST = 3
SECOND = 1
WEIGHT_MOVES = ((2, 0), (0, 2), (1, 3))

F32 = jnp.float32
BF16 = jnp.bfloat16
VMEM = pltpu.MemorySpace.VMEM
SMEM = pltpu.MemorySpace.SMEM


def exchange(values, axis):
    return lax.all_to_all(values, axis, split_axis=0, concat_axis=0, tiled=True)


def pick_rows(table, ids):
    onehot = (ids[:, None] == jnp.arange(table.shape[0], dtype=jnp.int32)[None, :]).astype(BF16)
    return jnp.dot(onehot, table, preferred_element_type=F32).astype(BF16)


def dot(a, b):
    return jnp.dot(a, b, preferred_element_type=F32)


def moved_down(values, rows):
    at = lax.broadcasted_iota(jnp.int32, values.shape, 0)
    return jnp.where(at < rows, 0.0, pltpu.roll(values, rows, 0))


def taps(parts, gap):
    return parts[0] + moved_down(parts[1], gap) + moved_down(parts[2], 2 * gap)


def ask_kernel(place, owner, row, cand, out):
    along = jnp.broadcast_to(owner[...].astype(F32), (128, WINDOW))
    down = jnp.transpose(jnp.concatenate([along, along], axis=1))[:WINDOW, :WINDOW]
    grid = (WINDOW, WINDOW)
    earlier = lax.broadcasted_iota(jnp.int32, grid, 0) < lax.broadcasted_iota(jnp.int32, grid, 1)
    slot = jnp.sum(jnp.where((down == along[:WINDOW]) & earlier, 1.0, 0.0), axis=0, keepdims=True)
    of_owner = along == lax.broadcasted_iota(jnp.int32, along.shape, 0).astype(F32)
    rows = row[...].astype(F32)
    lane = lax.broadcasted_iota(jnp.int32, (128, 128), 1)
    history = jnp.zeros((128, 128), F32)
    for k in range(CAP):
        column = jnp.sum(jnp.where(of_owner & (slot == k), rows, 0.0), axis=1, keepdims=True)
        history = jnp.where(lane == k, column, history)
    slots = cand[...].astype(F32)
    mp_index = place[2]
    chosen = jnp.where(
        mp_index == SECOND,
        slots[:CAP],
        jnp.where(mp_index == 0, slots[CAP:], jnp.concatenate([slots[6:], slots[6:]], axis=0)),
    )
    cands = jnp.transpose(jnp.concatenate([chosen, jnp.zeros((128 - CAP, 128), F32)], axis=0))
    out[...] = jnp.where(mp_index == FIRST, history, cands).astype(jnp.int32)[:, : out.shape[1]]


def pack_kernel(place, conv_a, conv_b, *outs):
    side = pl.multiple_of(place[0] * 256, 256)
    for (to_first, _), out in zip(WEIGHT_MOVES, outs):
        start = jnp.where(place[2] == to_first, 0, 2)
        for j in range(2):
            for k in range(3):
                out[j, pl.ds(k * 256, 256), :] = conv_a[start + j, k, pl.ds(side, 256), :]
                for half in range(2):
                    rows = pl.ds(768 + half * 384 + k * 128, 128)
                    out[j, rows, :] = conv_b[start + j, k, :, pl.ds(pl.multiple_of(side + half * 128, 128), 128)]


def block(hidden, j, gap, core_even, base, gain, conv_a, conv_b, mine, theirs):
    left, right = hidden[:, :256], hidden[:, 256:]
    at_mine = jnp.where(core_even, left, right)
    at_theirs = jnp.where(core_even, right, left)
    parts = []
    for k in range(3):
        rows = pl.ds(k * 256, 256)
        own = dot(hidden, conv_a[base + j, k])
        far = dot(at_mine, jnp.concatenate([w[j, rows, :] for w in mine], axis=1))
        far = far + dot(at_theirs, jnp.concatenate([w[j, rows, :] for w in theirs], axis=1))
        parts.append(jnp.concatenate([own, far], axis=1))
    rectified = jnp.maximum(taps(parts, gap), 0.0).astype(BF16)
    own_rect, far_rect = rectified[:, :QUARTER], rectified[:, QUARTER:]

    def columns(refs, k):
        return jnp.concatenate(
            [
                jnp.concatenate(
                    [w[j, pl.ds(768 + k * 128, 128), :], w[j, pl.ds(1152 + k * 128, 128), :]], axis=1
                )
                for w in refs
            ],
            axis=0,
        )

    own = taps([dot(own_rect, conv_b[base + j, k]) for k in range(3)], 2 * gap)
    z_mine = taps([dot(far_rect, columns(mine, k)) for k in range(3)], 2 * gap)
    z_theirs = taps([dot(far_rect, columns(theirs, k)) for k in range(3)], 2 * gap)
    far = jnp.concatenate(
        [jnp.where(core_even, z_mine, z_theirs), jnp.where(core_even, z_theirs, z_mine)], axis=1
    )
    summed = hidden.astype(F32) + own + far
    row_mean = jnp.mean(summed, axis=1, keepdims=True)
    row_msq = jnp.mean(summed * summed, axis=1, keepdims=True)
    row_var = row_msq - row_mean * row_mean
    return ((summed - row_mean) * lax.rsqrt(row_var + 1e-05) * gain).astype(BF16)


def two_blocks(hidden, stage, place, gains, conv_a, conv_b, mine, theirs):
    core_even = place[0] == 0
    base = place[1]
    for j, gap in ((0, 1), (1, 4)):
        gain = gains[pl.ds(2 * stage + j, 1), :]
        hidden = block(hidden, j, gap, core_even, base, gain, conv_a, conv_b, mine, theirs)
    return hidden


def first_kernel(place, hidden, gains, conv_a, conv_b, m0, m1, m2, t0, t1, t2, out):
    last = two_blocks(hidden[...], 0, place, gains, conv_a, conv_b, (m0, m1, m2), (t0, t1, t2))
    out[...] = last[LATE:]


def second_kernel(
    place, hidden, gains, conv_a, conv_b, m0, m1, m2, t0, t1, t2, w_out, rows_a, rows_b, rows_c, count, pos, out
):
    last = two_blocks(hidden[...], 1, place, gains, conv_a, conv_b, (m0, m1, m2), (t0, t1, t2))
    vec = dot(last[LATE - 16 :], w_out[...]).astype(BF16)

    def against(rows, per):
        scored = lax.dot_general(vec, rows[...], (((1,), (1,)), ((), ())), preferred_element_type=F32)[15:16]
        shape = (CPO, scored.shape[1])
        lane = lax.broadcasted_iota(jnp.int32, shape, 1)
        return jnp.broadcast_to(0.25 * scored, shape), lane % per

    owner_of, kept = [], []
    slot = lax.broadcasted_iota(jnp.int32, (CPO, 1), 0)
    first_slot = 0
    for rows, per in ((rows_a, 4), (rows_b, 2), (rows_c, 2)):
        scored, place_in = against(rows, per)
        kept.append(jnp.where(place_in + first_slot == slot, scored, 0.0))
        grid = (scored.shape[1], 128)
        owner_of.append(
            (lax.broadcasted_iota(jnp.int32, grid, 0) // per == lax.broadcasted_iota(jnp.int32, grid, 1)).astype(F32)
        )
        first_slot += per
    raw = jnp.dot(
        jnp.concatenate(kept, axis=1),
        jnp.concatenate(owner_of, axis=0),
        precision=lax.Precision.HIGHEST,
        preferred_element_type=F32,
    )
    valid = slot < count[...]
    total = jnp.sum(jnp.where(valid, jnp.exp(raw), 0.0), axis=(0, 1), keepdims=True)
    owner = lax.broadcasted_iota(jnp.int32, (1, 128), 1)
    positive = jnp.sum(jnp.where(owner == pos[0], raw[:1], 0.0), axis=(0, 1), keepdims=True)
    out[:CPO, :] = jnp.where(valid, raw, 0.0)
    out[CPO:, :] = jnp.broadcast_to(jnp.log(total) - positive, (CPO, 128))


def call(kernel, out_shape, operands, flops):
    in_smem = {0, len(operands) - 1} if kernel is second_kernel else {0}
    return pl.pallas_call(
        kernel,
        out_shape=out_shape,
        in_specs=[pl.BlockSpec(memory_space=SMEM if i in in_smem else VMEM) for i in range(len(operands))],
        out_specs=jax.tree.map(lambda _: pl.BlockSpec(memory_space=VMEM), out_shape),
        compiler_params=pltpu.CompilerParams(vmem_limit_bytes=24 * 1024 * 1024),
        cost_estimate=pl.CostEstimate(flops=flops, bytes_accessed=8 << 20, transcendentals=0),
    )(*operands)


def forward(
    item_table,
    history_owner,
    history_row,
    w_in,
    conv_a,
    conv_b,
    gains,
    w_out,
    cand_row,
    cand_count,
    pos_owner,
):
    dp_count = lax.axis_size("dp")
    mp_count = lax.axis_size("mp")
    dp_index = lax.axis_index("dp")
    mp_index = lax.axis_index("mp")
    base = jnp.where(mp_index == SECOND, 2, 0)
    place = jnp.stack([dp_index % 2, base, mp_index]).astype(jnp.int32)
    asks = call(
        ask_kernel,
        jax.ShapeDtypeStruct((dp_count, 16), jnp.int32),
        (place, history_owner.reshape(1, WINDOW), history_row.reshape(1, WINDOW), cand_row[0].T),
        1 << 20,
    )
    asks, pack_a, pack_b = lax.optimization_barrier((asks, conv_a, conv_b))
    asked = exchange(asks, "dp")[:, :CAP]

    sent = call(
        pack_kernel, [jax.ShapeDtypeStruct((2, 1536, 128), BF16)] * 3, (place, pack_a, pack_b), 1 << 20
    )
    mine, theirs = [], []
    for (to_first, to_second), half in zip(WEIGHT_MOVES, sent):
        mine.append(lax.ppermute(half, "mp", [(to_first, FIRST), (to_second, SECOND)]))
    for half in mine:
        theirs.append(lax.ppermute(half, "dp", [(i, i ^ 1) for i in range(dp_count)]))
    picked = pick_rows(item_table, asked.reshape(-1)).reshape(dp_count, CAP, -1)
    arrived = exchange(picked, "dp")
    arrived_rows = arrived.reshape(dp_count * CAP, -1)
    owner_ids = history_owner[:, 0]
    event = jnp.arange(WINDOW, dtype=jnp.int32)
    same = owner_ids[:, None] == owner_ids[None, :]
    slot = jnp.sum((same & (event[None, :] < event[:, None])).astype(jnp.int32), axis=1)
    embedded = pick_rows(arrived_rows, owner_ids * CAP + slot)
    hidden = jnp.dot(embedded, w_in, preferred_element_type=F32).astype(BF16)
    hidden = call(
        first_kernel,
        jax.ShapeDtypeStruct((LATE, C), BF16),
        (place, hidden, gains, conv_a, conv_b, *mine, *theirs),
        2 * 2 * 64 * 6 * 512 * 512,
    )
    hidden = lax.ppermute(hidden, "mp", [(FIRST, SECOND)])
    pair = arrived[:, :2]
    rows_b = lax.ppermute(pair, "mp", [(0, SECOND)]).reshape(2 * dp_count, -1)
    rows_c = lax.ppermute(pair, "mp", [(2, SECOND)]).reshape(2 * dp_count, -1)
    packed_out = call(
        second_kernel,
        jax.ShapeDtypeStruct((2 * CPO, dp_count), F32),
        (place, hidden, gains, conv_a, conv_b, *mine, *theirs, w_out, arrived_rows, rows_b, rows_c, cand_count, pos_owner),
        2 * 2 * 32 * 6 * 512 * 512,
    )
    shared = exchange(jnp.broadcast_to(packed_out[None], (mp_count,) + packed_out.shape), "mp")[SECOND]
    return (shared[:CPO].T[None], shared[CPO, :1])


def solution(mesh):
    return jax.shard_map(
        forward,
        mesh=mesh,
        in_specs=(
            P("dp", None),
            P(("dp", "mp"), None),
            P(("dp", "mp")),
            P(),
            P(None, None, None, "mp"),
            P(None, None, "mp", None),
            P(),
            P(),
            P("dp", None, None),
            P("dp", None),
            P("dp"),
        ),
        out_specs=(P("dp", None, None), P("dp")),
        check_vma=False,
    )
```

time: 144 us -> 122 us (0.85)
  blocking collectives: 67.4 us -> 42 us
  waiting for transfers between devices: 35.8 us -> 14.8 us
  local copies, waits for them, and re-layouts: 5.36 us -> 19.6 us
  starting transfers between devices: 13.8 us -> 27.5 us
  Pallas kernels: 0 us -> 11.7 us
  matrix products: 10.1 us -> 2.99 us
  other arithmetic: 6.03 us -> 0.26 us
  between operations: 4.15 us -> 1.53 us
    all_to_all x5 -> x2, blocking collectives: 67.4 us -> 42 us  [exchange(): return lax.all_to_all(values, axis, split_axis=0, concat_axis=0, tiled=True)]
    all_to_all x3 -> x1, waiting for transfers between devices: 35.8 us -> 14.8 us  [exchange(): return lax.all_to_all(values, axis, split_axis=0, concat_axis=0, tiled=True)]
    ppermute x0 -> x9, starting transfers between devices: none -> 19.6 us  [the longest x3 8.41 us: forward(): lax.ppermute(half, 'mp', [(to_first, FIRST), (to_second, SECOND)])]
    pallas_call x0 -> x4, Pallas kernels: none -> 11.7 us  [call(): pl.pallas_call(kernel, out_shape=out_shape, in_specs=[pl.BlockSpec(memory...]
    unnamed x16 -> x30, local copies, waits for them, and re-layouts: 0.66 us -> 10.5 us
    dot_general x27 -> x1, matrix products: 9.04 us -> 1.42 us  [forward(): hidden = jnp.dot(embedded, w_in, preferred_element_type=F32).astype(BF16)]
    all_to_all x3 -> x1, starting transfers between devices: 13.8 us -> 7.92 us  [exchange(): return lax.all_to_all(values, axis, split_axis=0, concat_axis=0, tiled=True)]
    reshape x2 -> x4, local copies, waits for them, and re-layouts: 0.82 us -> 6.17 us  [the longest x1 1.86 us: forward(): picked = pick_rows(item_table, asked.reshape(-1)).reshape(dp_count, CAP, -1)]
  transfers between devices with their start and end apart: 3 -> 10, of which waited for: 3 -> 1; matrix products, arithmetic and copies ran while one was open for 2% -> 9% of each run, Pallas kernels for 0% -> 4%
where the time goes in v2:
time: 122 us; the launch traced here: 120 us
  blocking collectives  42 us (34%)
  starting transfers between devices  27.5 us (23%)
  local copies, waits for them, and re-layouts  19.6 us (16%)
  waiting for transfers between devices  14.8 us (12%)
  Pallas kernels  11.7 us (10%)
  matrix products  2.99 us (2%)
  between operations  1.53 us (1%)
    all_to_all x2, blocking collectives, exchange(): return lax.all_to_all(values, axis, split_axis=0, concat_axis=0, tiled=True)  42 us
    all_to_all x1, waiting for transfers between devices, exchange(): return lax.all_to_all(values, axis, split_axis=0, concat_axis=0, tiled=True)  14.8 us
    pallas_call x4, Pallas kernels, call(): pl.pallas_call(kernel, out_shape=out_shape, in_specs=[pl.BlockSpec(memory...  11.7 us
    unnamed x30, local copies, waits for them, and re-layouts  10.5 us
    ppermute x3, starting transfers between devices, forward(): lax.ppermute(half, 'mp', [(to_first, FIRST), (to_second, SECOND)])  8.41 us
    all_to_all x1, starting transfers between devices, exchange(): return lax.all_to_all(values, axis, split_axis=0, concat_axis=0, tiled=True)  7.92 us
    ppermute x3, starting transfers between devices, forward(): lax.ppermute(half, 'dp', [(i, i ^ 1) for i in range(dp_count)])  6.36 us
  transfers between devices with their start and end apart: 10, of which 1 were waited for; matrix products, arithmetic and copies ran while one was open for 9% of the time, Pallas kernels for 4%

profile of v2, /device:TPU:24, one launch (start us, length us, event | category | flops | bytes accessed | tf_op | source)
XLA Modules:
  0.0 120.4 jit_solution(3011492217827360961)
XLA Ops:
  0.6 0.0 copy-start
  0.7 0.1 pad_add_fusion.place
  0.7 0.0 copy-start.10
  0.7 0.8 copy-done.10
  1.5 0.0 copy-start.11
  1.5 0.7 copy-done.11
  2.1 0.0 copy-start.12
  2.2 0.7 copy-done.12
  2.8 0.9 shard_map.122
  3.7 0.0 copy-start.1
  3.7 1.4 %copy-done.1 = bf16[4,3,512,128]{3,2,1,0:T(8,128)(2,1)S(1)} copy-done((bf16[4,3,512,128]{3,2,1,0:T(8,128)(2,1)S(1)}, bf16[4,3,512,128]{3,2,1,0:T(8,128)(2,1)}, u32[]{:S(2)}) %copy-start.1) | copy-done | bytes 1572888
  5.1 1.4 %copy-done.3 = bf16[4,3,128,512]{3,2,1,0:T(8,128)(2,1)S(1)} copy-done((bf16[4,3,128,512]{3,2,1,0:T(8,128)(2,1)S(1)}, bf16[4,3,128,512]{3,2,1,0:T(8,128)(2,1)}, u32[]{:S(2)}) %copy-start.3) | copy-done | bytes 1572888
  6.5 2.2 %shard_map.123 = (bf16[2,1536,128]{2,1,0:T(8,128)(2,1)}, bf16[2,1536,128]{2,1,0:T(8,128)(2,1)}, bf16[2,1536,128]{2,1,0:T(8,128)(2,1)}) custom-call(s32[3]{0:T(128)S(1)} %pad_add_fusion.place, bf16[4,3,512,128]{3,2,1,0:T(8,128)(2,1)S(1)} %copy-done.1, bf16[4,3,128,512]{3,2,1,0:T(8,128)(2,1)S(1)} %copy-done.3), custom_call_target="tpu_custom_call" | custom-call | flops 1048576 | bytes 8388608 | tf_op jit(solution)/shard_map/pallas_call | solution.py:174
  8.8 3.4 %collective-permute-start = (bf16[2,1536,128]{2,1,0:T(8,128)(2,1)}, bf16[2,1536,128]{2,1,0:T(8,128)(2,1)S(1)}, u32[]{:S(2)}, u32[]{:S(2)}) collective-permute-start(bf16[2,1536,128]{2,1,0:T(8,128)(2,1)} %get-tuple-element.11), channel_id=1, source_target_pairs={{2,3},{0,1},{6,7},{4,5},{10,11},{8,9},{14,15},{12,13},{18,19},{16,... | collective-permute-start | bytes 2359304 | tf_op jit(solution)/shard_map/ppermute | solution.py:217
  12.2 3.4 %collective-permute-start.1 = (bf16[2,1536,128]{2,1,0:T(8,128)(2,1)}, bf16[2,1536,128]{2,1,0:T(8,128)(2,1)}, u32[]{:S(2)}, u32[]{:S(2)}) collective-permute-start(bf16[2,1536,128]{2,1,0:T(8,128)(2,1)} %get-tuple-element.12), channel_id=1, source_target_pairs={{0,3},{2,1},{4,7},{6,5},{8,11},{10,9},{12,15},{14,13},{16,19},{18,... | collective-permute-start | bytes 2359304 | tf_op jit(solution)/shard_map/ppermute | solution.py:217
  15.6 1.6 %collective-permute-start.2 = (bf16[2,1536,128]{2,1,0:T(8,128)(2,1)}, bf16[2,1536,128]{2,1,0:T(8,128)(2,1)}, u32[]{:S(2)}, u32[]{:S(2)}) collective-permute-start(bf16[2,1536,128]{2,1,0:T(8,128)(2,1)} %get-tuple-element.13), channel_id=1, source_target_pairs={{1,3},{3,1},{5,7},{7,5},{9,11},{11,9},{13,15},{15,13},{17,19},{19,... | collective-permute-start | bytes 2359304 | tf_op jit(solution)/shard_map/ppermute | solution.py:217
  17.2 32.8 %all_to_all.22 = s32[128,1,16]{2,1,0:T(1,128)S(1)} all-to-all(s32[128,1,16]{2,1,0:T(1,128)S(1)} %bitcast.32), channel_id=1, replica_groups=mesh['dp'=128,'mp'=4] {'dp'}, dimensions={0} | all-to-all | bytes 16384 | tf_op jit(solution)/shard_map/all_to_all | solution.py:26
  50.0 0.1 eq.59
  50.1 0.0 copy-done
  50.1 0.0 copy-start.13
  50.1 1.6 %fusion.2 = bf16[512,256]{1,0:T(8,128)(2,1)} fusion(bf16[2048,256]{1,0:T(8,128)(2,1)S(1)} %copy-done, s32[512]{0:T(512)S(1)} %eq.59), kind=kOutput, calls=%fused_computation.3 | convolution fusion | flops 538050560 | bytes 1312768 | tf_op jit(solution)/shard_map/dot_general | solution.py:31
  51.7 0.0 copy-start.2
  51.7 1.9 %reshape.28 = bf16[128,4,256]{2,1,0:T(4,128)(2,1)} reshape(bf16[512,256]{1,0:T(8,128)(2,1)} %fusion.2) | data formatting | bytes 524288 | tf_op jit(solution)/shard_map/reshape | solution.py:220
  53.5 7.9 %all-to-all-start.1 = ((bf16[128,4,256]{2,1,0:T(4,128)(2,1)}), bf16[128,4,256]{2,1,0:T(4,128)(2,1)}, u32[]{:S(2)}, u32[]{:S(2)}) async-start(bf16[128,4,256]{2,1,0:T(4,128)(2,1)} %reshape.28), calls=%async_computation.1 | async-start | bytes 524288 | tf_op jit(solution)/shard_map/all_to_all | solution.py:26
  61.5 0.0 collective-permute-done.m0
  61.5 2.0 %collective-permute-start.3 = (bf16[2,1536,128]{2,1,0:T(8,128)(2,1)S(1)}, bf16[2,1536,128]{2,1,0:T(8,128)(2,1)}, u32[]{:S(2)}, u32[]{:S(2)}) collective-permute-start(bf16[2,1536,128]{2,1,0:T(8,128)(2,1)S(1)} %collective-permute-done.m0), channel_id=1, source_target_pairs={{0,4},{4,0},{8,12},{12,8},{16,20},{20,16},{24,28},{28,24},{32,36},... | collective-permute-start | bytes 2359304 | tf_op jit(solution)/shard_map/ppermute | solution.py:219
  63.5 0.0 collective-permute-done.1.m1
  63.5 2.3 %collective-permute-start.4 = (bf16[2,1536,128]{2,1,0:T(8,128)(2,1)}, bf16[2,1536,128]{2,1,0:T(8,128)(2,1)}, u32[]{:S(2)}, u32[]{:S(2)}) collective-permute-start(bf16[2,1536,128]{2,1,0:T(8,128)(2,1)} %collective-permute-done.1.m1), channel_id=1, source_target_pairs={{0,4},{4,0},{8,12},{12,8},{16,20},{20,16},{24,28},{28,24},{32,36},... | collective-permute-start | bytes 2359304 | tf_op jit(solution)/shard_map/ppermute | solution.py:219
  65.8 0.0 collective-permute-done.2.m2
  65.8 2.0 %collective-permute-start.5 = (bf16[2,1536,128]{2,1,0:T(8,128)(2,1)}, bf16[2,1536,128]{2,1,0:T(8,128)(2,1)}, u32[]{:S(2)}, u32[]{:S(2)}) collective-permute-start(bf16[2,1536,128]{2,1,0:T(8,128)(2,1)} %collective-permute-done.2.m2), channel_id=1, source_target_pairs={{0,4},{4,0},{8,12},{12,8},{16,20},{20,16},{24,28},{28,24},{32,36},... | collective-permute-start | bytes 2359304 | tf_op jit(solution)/shard_map/ppermute | solution.py:219
  67.9 0.0 copy-done.13
  67.9 0.2 convert_reduce_fusion
  68.1 14.8 %all-to-all-done.1 = bf16[128,4,256]{2,1,0:T(4,128)(2,1)} async-done(((bf16[128,4,256]{2,1,0:T(4,128)(2,1)}), bf16[128,4,256]{2,1,0:T(4,128)(2,1)}, u32[]{:S(2)}, u32[]{:S(2)}) %all-to-all-start.1) | async-done | bytes 262176 | tf_op jit(solution)/shard_map/all_to_all | solution.py:26
  82.9 1.7 %slice.26 = bf16[128,2,256]{2,1,0:T(2,128)(2,1)} slice(bf16[128,4,256]{2,1,0:T(4,128)(2,1)} %all-to-all-done.1), slice={[0:128], [0:2], [0:256]} | slice | bytes 262144 | tf_op jit(solution)/shard_map/slice | solution.py:236
  84.6 1.3 %collective-permute-start.8 = (bf16[128,2,256]{2,1,0:T(2,128)(2,1)}, bf16[128,2,256]{2,1,0:T(2,128)(2,1)}, u32[]{:S(2)}, u32[]{:S(2)}) collective-permute-start(bf16[128,2,256]{2,1,0:T(2,128)(2,1)} %slice.26), channel_id=1, source_target_pairs={{2,1},{6,5},{10,9},{14,13},{18,17},{22,21},{26,25},{30,29},{34,33}... | collective-permute-start | bytes 393224 | tf_op jit(solution)/shard_map/ppermute | solution.py:238
  85.9 2.3 %collective-permute-start.7 = (bf16[128,2,256]{2,1,0:T(2,128)(2,1)}, bf16[128,2,256]{2,1,0:T(2,128)(2,1)}, u32[]{:S(2)}, u32[]{:S(2)}) collective-permute-start(bf16[128,2,256]{2,1,0:T(2,128)(2,1)} %slice.26), channel_id=1, source_target_pairs={{0,1},{4,5},{8,9},{12,13},{16,17},{20,21},{24,25},{28,29},{32,33},... | collective-permute-start | bytes 393224 | tf_op jit(solution)/shard_map/ppermute | solution.py:237
  88.2 1.7 %reshape.29.rows_a = bf16[512,256]{1,0:T(8,128)(2,1)} reshape(bf16[128,4,256]{2,1,0:T(4,128)(2,1)} %all-to-all-done.1) | data formatting | bytes 524288 | tf_op jit(solution)/shard_map/reshape | solution.py:222
  89.9 0.0 copy-start.14
  89.9 1.4 %convolution_convert_fusion.hidden = bf16[64,512]{1,0:T(8,128)(2,1)S(1)} fusion(bf16[256,512]{1,0:T(8,128)(2,1)} %param.14, bf16[512,256]{1,0:T(8,128)(2,1)} %reshape.29.rows_a, s32[64]{0:T(128)S(1)} %fusion.6), kind=kOutput, calls=%fused_computation.4 | convolution fusion | flops 33636352 | bytes 590080 | tf_op jit(solution)/shard_map/dot_general | solution.py:228
  91.3 0.0 collective-permute-done.3.t0
  91.3 0.0 collective-permute-done.4.t1
  91.4 0.0 collective-permute-done.5.t2
  91.4 0.0 copy-done.2
  91.4 0.0 copy-done.9
  91.4 0.0 copy-start.4
  91.4 1.4 %copy-done.4 = bf16[4,3,128,512]{3,2,1,0:T(8,128)(2,1)S(1)} copy-done((bf16[4,3,128,512]{3,2,1,0:T(8,128)(2,1)S(1)}, bf16[4,3,128,512]{3,2,1,0:T(8,128)(2,1)}, u32[]{:S(2)}) %copy-start.4) | copy-done | bytes 1572888
  92.8 4.2 %shard_map.124 = bf16[32,512]{1,0:T(8,128)(2,1)} custom-call(s32[3]{0:T(128)S(1)} %pad_add_fusion.place, bf16[64,512]{1,0:T(8,128)(2,1)S(1)} %convolution_convert_fusion.hidden, f32[4,512]{1,0:T(4,128)S(1)} %copy-done.9, bf16[4,3,512,128]{3,2,1,0:T(8,128)(2,1)S(1)} %copy-done.2, bf16[4,3,128,512]{3,2,1,0:T(8,128)(2,1)S(1)} %copy-done.4, ...), custom_call_target="tpu_custom_call" | custom-call | flops 402653184 | bytes 8388608 | tf_op jit(solution)/shard_map/pallas_call | solution.py:174
  97.0 1.3 %collective-permute-start.6 = (bf16[32,512]{1,0:T(8,128)(2,1)}, bf16[32,512]{1,0:T(8,128)(2,1)}, u32[]{:S(2)}, u32[]{:S(2)}) collective-permute-start(bf16[32,512]{1,0:T(8,128)(2,1)} %shard_map.124), channel_id=1, source_target_pairs={{3,1},{7,5},{11,9},{15,13},{19,17},{23,21},{27,25},{31,29},{35,33}... | collective-permute-start | bytes 98312 | tf_op jit(solution)/shard_map/ppermute | solution.py:235
  98.9 0.0 collective-permute-done.8
  99.0 1.0 reshape.31.rows_c
  99.9 0.0 collective-permute-done.7
  99.9 1.6 %reshape.30.rows_b = bf16[256,256]{1,0:T(8,128)(2,1)} reshape(bf16[128,2,256]{2,1,0:T(2,128)(2,1)} %collective-permute-done.7) | data formatting | bytes 262144 | tf_op jit(solution)/shard_map/reshape | solution.py:237
  101.6 0.0 collective-permute-done.6.hidden
  101.6 0.0 copy-done.14
  101.6 0.0 copy-start.5
  101.6 1.4 %copy-done.5 = bf16[4,3,128,512]{3,2,1,0:T(8,128)(2,1)S(1)} copy-done((bf16[4,3,128,512]{3,2,1,0:T(8,128)(2,1)S(1)}, bf16[4,3,128,512]{3,2,1,0:T(8,128)(2,1)}, u32[]{:S(2)}) %copy-start.5) | copy-done | bytes 1572888
  103.0 0.0 copy-start.6
  103.0 0.9 copy-done.6
  103.9 0.9 copy-done.7
  104.8 0.9 copy-done.8
  105.8 4.3 %shard_map.125 = f32[16,128]{1,0:T(8,128)S(1)} custom-call(s32[3]{0:T(128)S(1)} %pad_add_fusion.place, bf16[32,512]{1,0:T(8,128)(2,1)} %collective-permute-done.6.hidden, f32[4,512]{1,0:T(4,128)S(1)} %copy-done.9, bf16[4,3,512,128]{3,2,1,0:T(8,128)(2,1)S(1)} %copy-done.2, bf16[4,3,128,512]{3,2,1,0:T(8,128)(2,1)S(1)} %copy-done.5, ...), custom_call_target="tpu_custom_call" | custom-call | flops 201326592 | bytes 8388608 | tf_op jit(solution)/shard_map/pallas_call | solution.py:174
  110.1 9.2 %all_to_all.23 = f32[4,16,128]{2,1,0:T(8,128)S(1)} all-to-all(f32[4,16,128]{2,1,0:T(8,128)S(1)} %broadcast_in_dim.4), channel_id=1, replica_groups=mesh['dp'=128,'mp'=4] {'mp'}, dimensions={0} | all-to-all | bytes 65536 | tf_op jit(solution)/shard_map/all_to_all | solution.py:26
  119.3 0.5 slice.29
  119.8 0.6 slice_bitcast_fusion.1
  (7 shorter events, 0.0 us)
Async XLA Ops:
  0.6 49.5 %copy-start = (bf16[2048,256]{1,0:T(8,128)(2,1)S(1)}, bf16[2048,256]{1,0:T(8,128)(2,1)}, u32[]{:S(2)}) copy-start(bf16[2048,256]{1,0:T(8,128)(2,1)} %param.11) | copy-start | bytes 3145732
  0.7 0.8 copy-start.10
  1.5 0.7 copy-start.11
  2.1 0.7 copy-start.12
  3.7 1.4 %copy-start.1 = (bf16[4,3,512,128]{3,2,1,0:T(8,128)(2,1)S(1)}, bf16[4,3,512,128]{3,2,1,0:T(8,128)(2,1)}, u32[]{:S(2)}) copy-start(bf16[4,3,512,128]{3,2,1,0:T(8,128)(2,1)} %conv_a.4) | copy-start | bytes 4718596
  5.1 1.4 %copy-start.3 = (bf16[4,3,128,512]{3,2,1,0:T(8,128)(2,1)S(1)}, bf16[4,3,128,512]{3,2,1,0:T(8,128)(2,1)}, u32[]{:S(2)}) copy-start(bf16[4,3,128,512]{3,2,1,0:T(8,128)(2,1)} %conv_b.4) | copy-start | bytes 4718596
  8.8 52.7 %collective-permute-start = (bf16[2,1536,128]{2,1,0:T(8,128)(2,1)}, bf16[2,1536,128]{2,1,0:T(8,128)(2,1)S(1)}, u32[]{:S(2)}, u32[]{:S(2)}) collective-permute-start(bf16[2,1536,128]{2,1,0:T(8,128)(2,1)} %get-tuple-element.11), channel_id=1, source_target_pairs={{2,3},{0,1},{6,7},{4,5},{10,11},{8,9},{14,15},{12,13},{18,19},{16,... | collective-permute-start | bytes 2359304 | tf_op jit(solution)/shard_map/ppermute | solution.py:217
  12.2 51.3 %collective-permute-start.1 = (bf16[2,1536,128]{2,1,0:T(8,128)(2,1)}, bf16[2,1536,128]{2,1,0:T(8,128)(2,1)}, u32[]{:S(2)}, u32[]{:S(2)}) collective-permute-start(bf16[2,1536,128]{2,1,0:T(8,128)(2,1)} %get-tuple-element.12), channel_id=1, source_target_pairs={{0,3},{2,1},{4,7},{6,5},{8,11},{10,9},{12,15},{14,13},{16,19},{18,... | collective-permute-start | bytes 2359304 | tf_op jit(solution)/shard_map/ppermute | solution.py:217
  15.6 50.3 %collective-permute-start.2 = (bf16[2,1536,128]{2,1,0:T(8,128)(2,1)}, bf16[2,1536,128]{2,1,0:T(8,128)(2,1)}, u32[]{:S(2)}, u32[]{:S(2)}) collective-permute-start(bf16[2,1536,128]{2,1,0:T(8,128)(2,1)} %get-tuple-element.13), channel_id=1, source_target_pairs={{1,3},{3,1},{5,7},{7,5},{9,11},{11,9},{13,15},{15,13},{17,19},{19,... | collective-permute-start | bytes 2359304 | tf_op jit(solution)/shard_map/ppermute | solution.py:217
  50.1 17.8 %copy-start.13 = (s32[64,1]{0,1:T(1,128)S(1)}, s32[64,1]{0,1:T(1,128)}, u32[]{:S(2)}) copy-start(s32[64,1]{0,1:T(1,128)} %param.12) | copy-start | bytes 772
  51.7 39.7 %copy-start.2 = (bf16[4,3,512,128]{3,2,1,0:T(8,128)(2,1)S(1)}, bf16[4,3,512,128]{3,2,1,0:T(8,128)(2,1)}, u32[]{:S(2)}) copy-start(bf16[4,3,512,128]{3,2,1,0:T(8,128)(2,1)} %conv_a.4) | copy-start | bytes 4718596
  51.7 39.7 %copy-start.9 = (f32[4,512]{1,0:T(4,128)S(1)}, f32[4,512]{1,0:T(4,128)}, u32[]{:S(2)}) copy-start(f32[4,512]{1,0:T(4,128)} %gains.3) | copy-start | bytes 24580
  53.5 29.4 %all-to-all-start.1 = ((bf16[128,4,256]{2,1,0:T(4,128)(2,1)}), bf16[128,4,256]{2,1,0:T(4,128)(2,1)}, u32[]{:S(2)}, u32[]{:S(2)}) async-start(bf16[128,4,256]{2,1,0:T(4,128)(2,1)} %reshape.28), calls=%async_computation.1 | async-start | bytes 524288 | tf_op jit(solution)/shard_map/all_to_all | solution.py:26
  61.5 29.9 %collective-permute-start.3 = (bf16[2,1536,128]{2,1,0:T(8,128)(2,1)S(1)}, bf16[2,1536,128]{2,1,0:T(8,128)(2,1)}, u32[]{:S(2)}, u32[]{:S(2)}) collective-permute-start(bf16[2,1536,128]{2,1,0:T(8,128)(2,1)S(1)} %collective-permute-done.m0), channel_id=1, source_target_pairs={{0,4},{4,0},{8,12},{12,8},{16,20},{20,16},{24,28},{28,24},{32,36},... | collective-permute-start | bytes 2359304 | tf_op jit(solution)/shard_map/ppermute | solution.py:219
  63.5 27.8 %collective-permute-start.4 = (bf16[2,1536,128]{2,1,0:T(8,128)(2,1)}, bf16[2,1536,128]{2,1,0:T(8,128)(2,1)}, u32[]{:S(2)}, u32[]{:S(2)}) collective-permute-start(bf16[2,1536,128]{2,1,0:T(8,128)(2,1)} %collective-permute-done.1.m1), channel_id=1, source_target_pairs={{0,4},{4,0},{8,12},{12,8},{16,20},{20,16},{24,28},{28,24},{32,36},... | collective-permute-start | bytes 2359304 | tf_op jit(solution)/shard_map/ppermute | solution.py:219
  65.8 25.5 %collective-permute-start.5 = (bf16[2,1536,128]{2,1,0:T(8,128)(2,1)}, bf16[2,1536,128]{2,1,0:T(8,128)(2,1)}, u32[]{:S(2)}, u32[]{:S(2)}) collective-permute-start(bf16[2,1536,128]{2,1,0:T(8,128)(2,1)} %collective-permute-done.2.m2), channel_id=1, source_target_pairs={{0,4},{4,0},{8,12},{12,8},{16,20},{20,16},{24,28},{28,24},{32,36},... | collective-permute-start | bytes 2359304 | tf_op jit(solution)/shard_map/ppermute | solution.py:219
  84.6 14.4 %collective-permute-start.8 = (bf16[128,2,256]{2,1,0:T(2,128)(2,1)}, bf16[128,2,256]{2,1,0:T(2,128)(2,1)}, u32[]{:S(2)}, u32[]{:S(2)}) collective-permute-start(bf16[128,2,256]{2,1,0:T(2,128)(2,1)} %slice.26), channel_id=1, source_target_pairs={{2,1},{6,5},{10,9},{14,13},{18,17},{22,21},{26,25},{30,29},{34,33}... | collective-permute-start | bytes 393224 | tf_op jit(solution)/shard_map/ppermute | solution.py:238
  85.9 14.0 %collective-permute-start.7 = (bf16[128,2,256]{2,1,0:T(2,128)(2,1)}, bf16[128,2,256]{2,1,0:T(2,128)(2,1)}, u32[]{:S(2)}, u32[]{:S(2)}) collective-permute-start(bf16[128,2,256]{2,1,0:T(2,128)(2,1)} %slice.26), channel_id=1, source_target_pairs={{0,1},{4,5},{8,9},{12,13},{16,17},{20,21},{24,25},{28,29},{32,33},... | collective-permute-start | bytes 393224 | tf_op jit(solution)/shard_map/ppermute | solution.py:237
  89.9 11.7 %copy-start.14 = (s32[1,128]{1,0:T(1,128)S(1)}, s32[1,128]{1,0:T(1,128)}, u32[]{:S(2)}) copy-start(s32[1,128]{1,0:T(1,128)} %count.1) | copy-start | bytes 1540
  91.4 1.4 %copy-start.4 = (bf16[4,3,128,512]{3,2,1,0:T(8,128)(2,1)S(1)}, bf16[4,3,128,512]{3,2,1,0:T(8,128)(2,1)}, u32[]{:S(2)}) copy-start(bf16[4,3,128,512]{3,2,1,0:T(8,128)(2,1)} %conv_b.4) | copy-start | bytes 4718596
  97.0 4.5 %collective-permute-start.6 = (bf16[32,512]{1,0:T(8,128)(2,1)}, bf16[32,512]{1,0:T(8,128)(2,1)}, u32[]{:S(2)}, u32[]{:S(2)}) collective-permute-start(bf16[32,512]{1,0:T(8,128)(2,1)} %shard_map.124), channel_id=1, source_target_pairs={{3,1},{7,5},{11,9},{15,13},{19,17},{23,21},{27,25},{31,29},{35,33}... | collective-permute-start | bytes 98312 | tf_op jit(solution)/shard_map/ppermute | solution.py:235
  101.6 1.4 %copy-start.5 = (bf16[4,3,128,512]{3,2,1,0:T(8,128)(2,1)S(1)}, bf16[4,3,128,512]{3,2,1,0:T(8,128)(2,1)}, u32[]{:S(2)}) copy-start(bf16[4,3,128,512]{3,2,1,0:T(8,128)(2,1)} %conv_b.4) | copy-start | bytes 4718596
  103.0 0.9 copy-start.6
  103.9 0.9 copy-start.7
  104.8 0.9 copy-start.8

commit v3 on v2

v3 whole, which is shorter than its diff:
```python
import jax
import jax.numpy as jnp
from jax import lax
from jax.experimental import pallas as pl
from jax.experimental.pallas import tpu as pltpu
from jax.sharding import PartitionSpec as P


C = 512
QUARTER = 128
BLOCKS = 4
CAP = 4
CPO = 8
WINDOW = 64
LATE = 32
FIRST = 3
SECOND = 1
WEIGHT_MOVES = ((2, 0), (0, 2), (1, 3))

F32 = jnp.float32
BF16 = jnp.bfloat16
VMEM = pltpu.MemorySpace.VMEM
SMEM = pltpu.MemorySpace.SMEM
HBM = pltpu.MemorySpace.HBM
MIB = 1024 * 1024
WEIGHTS = (2, 4, 3, 128, 128)


def exchange(values, axis):
    return lax.all_to_all(values, axis, split_axis=0, concat_axis=0, tiled=True)


def dot(a, b):
    return jnp.dot(a, b, preferred_element_type=F32)


def dot_t(a, b):
    return lax.dot_general(a, b, (((1,), (1,)), ((), ())), preferred_element_type=F32)


def iota(shape, axis):
    return lax.broadcasted_iota(jnp.int32, shape, axis)


def core_of():
    return lax.rem(lax.axis_index("dp"), 2)


def start_all(copies):
    for copy in copies:
        copy.start()


def wait_all(copies):
    for copy in copies:
        copy.wait()


def moved_down(values, rows):
    return jnp.where(iota(values.shape, 0) < rows, 0.0, pltpu.roll(values, rows, 0))


def taps(parts, gap):
    return parts[0] + moved_down(parts[1], gap) + moved_down(parts[2], 2 * gap)


def ask_kernel(owner, row, cand, out, code, owner_v, row_v, cand_v, sems):
    copies = [
        pltpu.make_async_copy(owner, owner_v, sems.at[0]),
        pltpu.make_async_copy(row, row_v, sems.at[1]),
        pltpu.make_async_copy(cand, cand_v, sems.at[2]),
    ]
    start_all(copies)
    wait_all(copies)
    along = jnp.broadcast_to(owner_v[...].astype(F32), (128, WINDOW))
    down = jnp.transpose(jnp.concatenate([along, along], axis=1))[:WINDOW, :WINDOW]
    grid = (WINDOW, WINDOW)
    same = down == along[:WINDOW]
    first, second = iota(grid, 0), iota(grid, 1)
    slot = jnp.sum(jnp.where(same & (first < second), 1.0, 0.0), axis=0, keepdims=True)
    slot_down = jnp.sum(jnp.where(same & (second < first), 1.0, 0.0), axis=1, keepdims=True)
    code[...] = jnp.broadcast_to(8.0 * down[:, :1] + slot_down, (WINDOW, 128)).astype(jnp.int32)
    of_owner = along == iota(along.shape, 0).astype(F32)
    rows = row_v[...].astype(F32)
    lane = iota((128, 128), 1)
    history = jnp.zeros((128, 128), F32)
    for k in range(CAP):
        column = jnp.sum(jnp.where(of_owner & (slot == k), rows, 0.0), axis=1, keepdims=True)
        history = jnp.where(lane == k, column, history)
    slots = cand_v[...].astype(F32)
    mp_index = lax.axis_index("mp")
    chosen = jnp.where(mp_index == SECOND, slots[:CAP], slots[CAP:])
    cands = jnp.transpose(jnp.concatenate([chosen, jnp.zeros((128 - CAP, 128), F32)], axis=0))
    out[...] = jnp.where(mp_index == FIRST, history, cands).astype(jnp.int32)[:, : out.shape[1]]


def pack_kernel(conv_a, conv_b, out_0, out_1, out_2, packed, sems):
    side = pl.multiple_of(core_of() * 256, 256)
    mp_index = lax.axis_index("mp")
    loads = []
    for half in range(2):
        at = pl.ds(pl.multiple_of(side + half * 128, 128), 128)
        loads.append(pltpu.make_async_copy(conv_a.at[:, :, at, :], packed.at[:, half], sems.at[half]))
        loads.append(pltpu.make_async_copy(conv_b.at[:, :, :, at], packed.at[:, 2 + half], sems.at[2 + half]))
    start_all(loads)
    wait_all(loads)
    stores = []
    for i, ((to_first, _), out) in enumerate(zip(WEIGHT_MOVES, (out_0, out_1, out_2))):
        start = jnp.where(mp_index == to_first, 0, 2)
        stores.append(pltpu.make_async_copy(packed.at[pl.ds(start, 2)], out, sems.at[4 + i]))
    start_all(stores)
    wait_all(stores)


def pick_kernel(asked, table, out):
    count = out.shape[0]
    spread = (iota((count, 128), 0) // 8 == iota((count, 128), 1)).astype(BF16)
    wanted = asked[...]
    high = dot(spread, (wanted // 64).astype(F32).astype(BF16))
    low = dot(spread, (wanted % 64).astype(F32).astype(BF16))
    here = iota(high.shape, 0) % 4 == iota(high.shape, 1)
    ids = jnp.sum(jnp.where(here, 64.0 * high + low, 0.0), axis=1, keepdims=True).astype(jnp.int32)
    rows = 256
    for at in range(0, count, rows):
        onehot = (ids[at : at + rows] == iota((rows, table.shape[0]), 1)).astype(F32).astype(BF16)
        both = dot(onehot, table[...])
        second = iota((rows, 128), 0) % 8 >= 4
        out[at : at + rows, :] = jnp.where(second, both[:, 128:], both[:, :128]).astype(BF16)


def block(hidden, j, gap, core_even, gain, conv_a, conv_b, mine, theirs):
    left, right = hidden[:, :256], hidden[:, 256:]
    at_mine = jnp.where(core_even, left, right)
    at_theirs = jnp.where(core_even, right, left)

    def split(ref, k):
        both = [jnp.concatenate([ref[i, j, half, k] for i in range(3)], axis=1) for half in range(2)]
        return jnp.concatenate(both, axis=0)

    parts = []
    for k in range(3):
        own = dot(hidden, conv_a[j, k])
        far = dot(at_mine, split(mine, k)) + dot(at_theirs, split(theirs, k))
        parts.append(jnp.concatenate([own, far], axis=1))
    rectified = jnp.maximum(taps(parts, gap), 0.0).astype(BF16)
    own_rect, far_rect = rectified[:, :QUARTER], rectified[:, QUARTER:]

    def columns(ref, k):
        return jnp.concatenate(
            [jnp.concatenate([ref[i, j, 2, k], ref[i, j, 3, k]], axis=1) for i in range(3)], axis=0
        )

    own = taps([dot(own_rect, conv_b[j, k]) for k in range(3)], 2 * gap)
    z_mine = taps([dot(far_rect, columns(mine, k)) for k in range(3)], 2 * gap)
    z_theirs = taps([dot(far_rect, columns(theirs, k)) for k in range(3)], 2 * gap)
    far = jnp.concatenate(
        [jnp.where(core_even, z_mine, z_theirs), jnp.where(core_even, z_theirs, z_mine)], axis=1
    )
    summed = hidden.astype(F32) + own + far
    row_mean = jnp.mean(summed, axis=1, keepdims=True)
    row_msq = jnp.mean(summed * summed, axis=1, keepdims=True)
    row_var = row_msq - row_mean * row_mean
    return ((summed - row_mean) * lax.rsqrt(row_var + 1e-05) * gain).astype(BF16)


def weight_copies(conv_a, conv_b, moved, own_a, own_b, mine, theirs, sems):
    base = jnp.where(lax.axis_index("mp") == SECOND, 2, 0)
    copies = []
    for j in range(2):
        pairs = [(conv_a.at[base + j], own_a.at[j]), (conv_b.at[base + j], own_b.at[j])]
        pairs += [(moved[i].at[j], mine.at[i, j]) for i in range(3)]
        pairs += [(moved[3 + i].at[j], theirs.at[i, j]) for i in range(3)]
        copies.append([pltpu.make_async_copy(a, b, sems.at[8 * j + n]) for n, (a, b) in enumerate(pairs)])
    return copies


WEIGHT_SCRATCH = (
    pltpu.VMEM((2, 3, C, QUARTER), BF16),
    pltpu.VMEM((2, 3, QUARTER, C), BF16),
    pltpu.VMEM((3,) + WEIGHTS, BF16),
    pltpu.VMEM((3,) + WEIGHTS, BF16),
    pltpu.SemaphoreType.DMA((16,)),
)


def two_blocks(hidden, stage, gains, copies, own_a, own_b, mine, theirs):
    core_even = core_of() == 0
    for j, gap in ((0, 1), (1, 4)):
        wait_all(copies[j])
        gain = gains[pl.ds(2 * stage + j, 1), :]
        hidden = block(hidden, j, gap, core_even, gain, own_a, own_b, mine, theirs)
    return hidden


def first_kernel(arrived, code, w_in, gains, conv_a, conv_b, m0, m1, m2, t0, t1, t2, out, own_a, own_b, mine, theirs, sems):
    copies = weight_copies(conv_a, conv_b, (m0, m1, m2, t0, t1, t2), own_a, own_b, mine, theirs, sems)
    start_all(copies[0])
    start_all(copies[1])
    at = code[:, :1]
    lanes = iota((WINDOW, arrived.shape[0]), 1)
    picked = [dot((at + 4 * half == lanes).astype(F32).astype(BF16), arrived[...]) for half in range(2)]
    embedded = jnp.concatenate(picked, axis=1).astype(BF16)
    hidden = dot(embedded, w_in[...]).astype(BF16)
    out[...] = two_blocks(hidden, 0, gains, copies, own_a, own_b, mine, theirs)[LATE:]


def second_kernel(
    pos, hidden, gains, conv_a, conv_b, m0, m1, m2, t0, t1, t2, w_out, near, far, count, out, own_a, own_b, mine, theirs, sems
):
    copies = weight_copies(conv_a, conv_b, (m0, m1, m2, t0, t1, t2), own_a, own_b, mine, theirs, sems)
    start_all(copies[0])
    start_all(copies[1])
    last = two_blocks(hidden[...], 1, gains, copies, own_a, own_b, mine, theirs)
    vec = dot(last[LATE - 16 :], w_out[...]).astype(BF16)
    grid = (CPO, near.shape[0])
    second = iota((1, near.shape[0]), 1) % 8 >= 4

    def scored(rows):
        halves = [dot_t(vec[:, at : at + 128], rows[...])[15:16] for at in (0, 128)]
        return jnp.broadcast_to(0.25 * jnp.where(second, halves[1], halves[0]), grid)

    slot, lane = iota(grid, 0), iota(grid, 1)
    kept = jnp.where(lane % 4 == slot % 4, jnp.where(slot < CAP, scored(near), scored(far)), 0.0)
    pieces, rest = [], kept
    for _ in range(3):
        piece = rest.astype(BF16)
        pieces.append(piece.astype(F32))
        rest = rest - piece.astype(F32)
    owners = (iota((grid[1], 128), 0) // 8 == iota((grid[1], 128), 1)).astype(F32).astype(BF16)
    sums = dot(jnp.concatenate(pieces, axis=0).astype(BF16), owners)
    raw = sums[:CPO] + sums[CPO : 2 * CPO] + sums[2 * CPO :]
    valid = iota(raw.shape, 0) < count[...]
    total = jnp.sum(jnp.where(valid, jnp.exp(raw), 0.0), axis=(0, 1), keepdims=True)
    positive = jnp.sum(jnp.where(iota((1, 128), 1) == pos[0], raw[:1], 0.0), axis=(0, 1), keepdims=True)
    out[:CPO, :] = jnp.where(valid, raw, 0.0)
    out[CPO:, :] = jnp.broadcast_to(jnp.log(total) - positive, (CPO, 128))


def call(kernel, out_shape, operands, spaces, out_space, scratch, limit):
    return pl.pallas_call(
        kernel,
        out_shape=out_shape,
        in_specs=[pl.BlockSpec(memory_space=space) for space in spaces],
        out_specs=jax.tree.map(lambda _: pl.BlockSpec(memory_space=out_space), out_shape),
        scratch_shapes=scratch,
        compiler_params=pltpu.CompilerParams(vmem_limit_bytes=limit * MIB),
        cost_estimate=pl.CostEstimate(flops=1 << 28, bytes_accessed=8 << 20, transcendentals=0),
    )(*operands)


def forward(
    item_table,
    history_owner,
    history_row,
    w_in,
    conv_a,
    conv_b,
    gains,
    w_out,
    cand_row,
    cand_count,
    pos_owner,
):
    dp_count = lax.axis_size("dp")
    mp_count = lax.axis_size("mp")
    asks, code = call(
        ask_kernel,
        [jax.ShapeDtypeStruct((dp_count, 16), jnp.int32), jax.ShapeDtypeStruct((WINDOW, 128), jnp.int32)],
        (history_owner.reshape(1, WINDOW), history_row.reshape(1, WINDOW), cand_row[0].T),
        (HBM, HBM, HBM),
        VMEM,
        [
            pltpu.VMEM((1, WINDOW), jnp.int32),
            pltpu.VMEM((1, WINDOW), jnp.int32),
            pltpu.VMEM((CPO, 128), jnp.int32),
            pltpu.SemaphoreType.DMA((3,)),
        ],
        60,
    )
    asks, pack_a, pack_b = lax.optimization_barrier((asks, conv_a, conv_b))
    asked = exchange(asks, "dp")

    sent = call(
        pack_kernel,
        [jax.ShapeDtypeStruct(WEIGHTS, BF16)] * 3,
        (pack_a, pack_b),
        (HBM, HBM),
        HBM,
        [pltpu.VMEM((BLOCKS, 4, 3, 128, 128), BF16), pltpu.SemaphoreType.DMA((7,))],
        60,
    )
    moved = []
    for (to_first, to_second), half in zip(WEIGHT_MOVES, sent):
        moved.append(lax.ppermute(half, "mp", [(to_first, FIRST), (to_second, SECOND)]))
    for half in moved[:3]:
        moved.append(lax.ppermute(half, "dp", [(i, i ^ 1) for i in range(dp_count)]))

    picked = call(
        pick_kernel,
        jax.ShapeDtypeStruct((dp_count * 8, 128), BF16),
        (asked, item_table),
        (VMEM, VMEM),
        VMEM,
        [],
        60,
    )
    arrived = exchange(picked, "dp")
    far = lax.ppermute(arrived, "mp", [(0, SECOND)])
    hidden = call(
        first_kernel,
        jax.ShapeDtypeStruct((LATE, C), BF16),
        (arrived, code, w_in, gains, conv_a, conv_b, *moved),
        (VMEM,) * 4 + (HBM,) * 8,
        VMEM,
        WEIGHT_SCRATCH,
        24,
    )
    hidden = lax.ppermute(hidden, "mp", [(FIRST, SECOND)])
    packed_out = call(
        second_kernel,
        jax.ShapeDtypeStruct((2 * CPO, dp_count), F32),
        (pos_owner, hidden, gains, conv_a, conv_b, *moved, w_out, arrived, far, cand_count),
        (SMEM, VMEM, VMEM) + (HBM,) * 8 + (VMEM,) * 4,
        VMEM,
        WEIGHT_SCRATCH,
        24,
    )
    shared = exchange(jnp.broadcast_to(packed_out[None], (mp_count,) + packed_out.shape), "mp")[SECOND]
    return (shared[:CPO].T[None], shared[CPO, :1])


def solution(mesh):
    return jax.shard_map(
        forward,
        mesh=mesh,
        in_specs=(
            P("dp", None),
            P(("dp", "mp"), None),
            P(("dp", "mp")),
            P(),
            P(None, None, None, "mp"),
            P(None, None, "mp", None),
            P(),
            P(),
            P("dp", None, None),
            P("dp", None),
            P("dp"),
        ),
        out_specs=(P("dp", None, None), P("dp")),
        check_vma=False,
    )
```

time: 122 us -> 105 us (0.86)
  local copies, waits for them, and re-layouts: 19.6 us -> 2.09 us
  Pallas kernels: 11.7 us -> 16.4 us
  starting transfers between devices: 27.5 us -> 24.1 us
  matrix products: 2.99 us -> 0 us
  blocking collectives: 42 us -> 44.6 us
    unnamed x30 -> x16, local copies, waits for them, and re-layouts: 10.5 us -> 0.98 us
    reshape x4 -> x0, local copies, waits for them, and re-layouts: 6.17 us -> none  [the longest x1 1.86 us: forward(): picked = pick_rows(item_table, asked.reshape(-1)).reshape(dp_count, CAP, -1)]
    pallas_call x4 -> x5, Pallas kernels: 11.7 us -> 16.4 us  [call(): pl.pallas_call(kernel, out_shape=out_shape, in_specs=[pl.BlockSpec(memory...]
    dot_general x2 -> x0, matrix products: 2.99 us -> none  [the longest x1 1.57 us: pick_rows(): return jnp.dot(onehot, table, preferred_element_type=F32).astype(BF16)]
    all_to_all x2, blocking collectives: 42 us -> 44.6 us  [exchange(): return lax.all_to_all(values, axis, split_axis=0, concat_axis=0, tiled=True)]
    ppermute x2 -> x1, starting transfers between devices: 3.57 us -> 1.65 us  [forward(): far = lax.ppermute(arrived, 'mp', [(0, SECOND)])]
    slice x1 -> x0, local copies, waits for them, and re-layouts: 1.7 us -> none  [forward(): pair = arrived[:, :2]]
  transfers between devices with their start and end apart: 10 -> 9, of which waited for: 1 -> 1; matrix products, arithmetic and copies ran while one was open for 9% -> 0% of each run, Pallas kernels for 4% -> 7%
where the time goes in v3:
time: 105 us; the launch traced here: 104 us
  blocking collectives  44.6 us (42%)
  starting transfers between devices  24.1 us (23%)
  Pallas kernels  16.4 us (16%)
  waiting for transfers between devices  15.4 us (15%)
  local copies, waits for them, and re-layouts  2.09 us (2%)
  between operations  1.53 us (1%)
    all_to_all x2, blocking collectives, exchange(): return lax.all_to_all(values, axis, split_axis=0, concat_axis=0, tiled=True)  44.6 us
    pallas_call x5, Pallas kernels, call(): pl.pallas_call(kernel, out_shape=out_shape, in_specs=[pl.BlockSpec(memory...  16.4 us
    all_to_all x1, waiting for transfers between devices, exchange(): return lax.all_to_all(values, axis, split_axis=0, concat_axis=0, tiled=True)  15.4 us
    ppermute x3, starting transfers between devices, forward(): lax.ppermute(half, 'mp', [(to_first, FIRST), (to_second, SECOND)])  8.55 us
    all_to_all x1, starting transfers between devices, exchange(): return lax.all_to_all(values, axis, split_axis=0, concat_axis=0, tiled=True)  6.86 us
    ppermute x3, starting transfers between devices, forward(): lax.ppermute(half, 'dp', [(i, i ^ 1) for i in range(dp_count)])  6.36 us
  transfers between devices with their start and end apart: 9, of which 1 were waited for; matrix products, arithmetic and copies ran while one was open for 0% of the time, Pallas kernels for 7%

profile of v3, /device:TPU:24, one launch (start us, length us, event | category | flops | bytes accessed | tf_op | source)
XLA Modules:
  0.0 104.1 jit_solution(14720750298068778464)
XLA Ops:
  0.6 1.8 %shard_map.122 = (s32[128,16]{1,0:T(8,128)}, s32[64,128]{1,0:T(8,128)}) custom-call(s32[1,64]{1,0:T(1,128)} %bitcast.27, s32[1,64]{1,0:T(1,128)} %bitcast.28, s32[8,128]{1,0:T(8,128)} %bitcast.26), custom_call_target="tpu_custom_call" | custom-call | flops 268435456 | bytes 8388608 | tf_op jit(solution)/shard_map/pallas_call | solution.py:240
  2.4 0.0 copy-start.7
  2.4 0.0 copy-start.1
  2.4 3.0 %shard_map.124 = (bf16[2,4,3,128,128]{4,3,2,1,0:T(8,128)(2,1)}, bf16[2,4,3,128,128]{4,3,2,1,0:T(8,128)(2,1)}, bf16[2,4,3,128,128]{4,3,2,1,0:T(8,128)(2,1)}) custom-call(bf16[4,3,512,128]{3,2,1,0:T(8,128)(2,1)} %conv_a.4, bf16[4,3,128,512]{3,2,1,0:T(8,128)(2,1)} %conv_b.4), custom_call_target="tpu_custom_call" | custom-call | flops 268435456 | bytes 8388608 | tf_op jit(solution)/shard_map/pallas_call | solution.py:240
  5.4 0.0 copy-start
  5.4 0.0 copy-start.4
  5.4 0.0 copy-start.5
  5.4 4.4 %collective-permute-start = (bf16[2,4,3,128,128]{4,3,2,1,0:T(8,128)(2,1)}, bf16[2,4,3,128,128]{4,3,2,1,0:T(8,128)(2,1)}, u32[]{:S(2)}, u32[]{:S(2)}) collective-permute-start(bf16[2,4,3,128,128]{4,3,2,1,0:T(8,128)(2,1)} %get-tuple-element.15), channel_id=1, source_target_pairs={{2,3},{0,1},{6,7},{4,5},{10,11},{8,9},{14,15},{12,13},{18,19},{16,... | collective-permute-start | bytes 2359304 | tf_op jit(solution)/shard_map/ppermute | solution.py:294
  9.9 2.6 %collective-permute-start.1 = (bf16[2,4,3,128,128]{4,3,2,1,0:T(8,128)(2,1)}, bf16[2,4,3,128,128]{4,3,2,1,0:T(8,128)(2,1)}, u32[]{:S(2)}, u32[]{:S(2)}) collective-permute-start(bf16[2,4,3,128,128]{4,3,2,1,0:T(8,128)(2,1)} %get-tuple-element.16), channel_id=1, source_target_pairs={{0,3},{2,1},{4,7},{6,5},{8,11},{10,9},{12,15},{14,13},{16,19},{18,... | collective-permute-start | bytes 2359304 | tf_op jit(solution)/shard_map/ppermute | solution.py:294
  12.4 1.5 %collective-permute-start.2 = (bf16[2,4,3,128,128]{4,3,2,1,0:T(8,128)(2,1)}, bf16[2,4,3,128,128]{4,3,2,1,0:T(8,128)(2,1)}, u32[]{:S(2)}, u32[]{:S(2)}) collective-permute-start(bf16[2,4,3,128,128]{4,3,2,1,0:T(8,128)(2,1)} %get-tuple-element.17), channel_id=1, source_target_pairs={{1,3},{3,1},{5,7},{7,5},{9,11},{11,9},{13,15},{15,13},{17,19},{19,... | collective-permute-start | bytes 2359304 | tf_op jit(solution)/shard_map/ppermute | solution.py:294
  14.0 0.0 copy-done.7
  14.0 32.8 %all_to_all.27 = s32[128,1,16]{2,1,0:T(1,128)} all-to-all(s32[128,1,16]{2,1,0:T(1,128)S(1)} %bitcast.25), channel_id=1, replica_groups=mesh['dp'=128,'mp'=4] {'dp'}, dimensions={0} | all-to-all | bytes 16384 | tf_op jit(solution)/shard_map/all_to_all | solution.py:30
  46.8 3.5 %shard_map.123 = bf16[1024,128]{1,0:T(8,128)(2,1)} custom-call(s32[128,16]{1,0:T(8,128)} %bitcast.24, bf16[2048,256]{1,0:T(8,128)(2,1)} %table.1), custom_call_target="tpu_custom_call" | custom-call | flops 268435456 | bytes 8388608 | tf_op jit(solution)/shard_map/pallas_call | solution.py:240
  50.3 6.9 %all-to-all-start.1 = ((bf16[128,8,128]{2,1,0:T(8,128)(2,1)}), bf16[128,8,128]{2,1,0:T(8,128)(2,1)S(1)}, u32[]{:S(2)}, u32[]{:S(2)}) async-start(bf16[128,8,128]{2,1,0:T(8,128)(2,1)} %bitcast.23), calls=%async_computation.1 | async-start | bytes 524288 | tf_op jit(solution)/shard_map/all_to_all | solution.py:30
  57.2 0.0 collective-permute-done.m0
  57.2 2.0 %collective-permute-start.3 = (bf16[2,4,3,128,128]{4,3,2,1,0:T(8,128)(2,1)}, bf16[2,4,3,128,128]{4,3,2,1,0:T(8,128)(2,1)}, u32[]{:S(2)}, u32[]{:S(2)}) collective-permute-start(bf16[2,4,3,128,128]{4,3,2,1,0:T(8,128)(2,1)} %collective-permute-done.m0), channel_id=1, source_target_pairs={{0,4},{4,0},{8,12},{12,8},{16,20},{20,16},{24,28},{28,24},{32,36},... | collective-permute-start | bytes 2359304 | tf_op jit(solution)/shard_map/ppermute | solution.py:296
  59.2 0.0 collective-permute-done.1.m1
  59.2 2.3 %collective-permute-start.4 = (bf16[2,4,3,128,128]{4,3,2,1,0:T(8,128)(2,1)}, bf16[2,4,3,128,128]{4,3,2,1,0:T(8,128)(2,1)}, u32[]{:S(2)}, u32[]{:S(2)}) collective-permute-start(bf16[2,4,3,128,128]{4,3,2,1,0:T(8,128)(2,1)} %collective-permute-done.1.m1), channel_id=1, source_target_pairs={{0,4},{4,0},{8,12},{12,8},{16,20},{20,16},{24,28},{28,24},{32,36},... | collective-permute-start | bytes 2359304 | tf_op jit(solution)/shard_map/ppermute | solution.py:296
  61.5 0.0 collective-permute-done.2.m2
  61.5 2.0 %collective-permute-start.5 = (bf16[2,4,3,128,128]{4,3,2,1,0:T(8,128)(2,1)}, bf16[2,4,3,128,128]{4,3,2,1,0:T(8,128)(2,1)}, u32[]{:S(2)}, u32[]{:S(2)}) collective-permute-start(bf16[2,4,3,128,128]{4,3,2,1,0:T(8,128)(2,1)} %collective-permute-done.2.m2), channel_id=1, source_target_pairs={{0,4},{4,0},{8,12},{12,8},{16,20},{20,16},{24,28},{28,24},{32,36},... | collective-permute-start | bytes 2359304 | tf_op jit(solution)/shard_map/ppermute | solution.py:296
  63.6 15.4 %all-to-all-done.1 = bf16[128,8,128]{2,1,0:T(8,128)(2,1)S(1)} async-done(((bf16[128,8,128]{2,1,0:T(8,128)(2,1)}), bf16[128,8,128]{2,1,0:T(8,128)(2,1)S(1)}, u32[]{:S(2)}, u32[]{:S(2)}) %all-to-all-start.1) | async-done | bytes 262176 | tf_op jit(solution)/shard_map/all_to_all | solution.py:30
  79.0 1.6 %collective-permute-start.7 = (bf16[1024,128]{1,0:T(8,128)(2,1)S(1)}, bf16[1024,128]{1,0:T(8,128)(2,1)S(1)}, u32[]{:S(2)}, u32[]{:S(2)}) collective-permute-start(bf16[1024,128]{1,0:T(8,128)(2,1)S(1)} %bitcast.20), channel_id=1, source_target_pairs={{0,1},{4,5},{8,9},{12,13},{16,17},{20,21},{24,25},{28,29},{32,33},... | collective-permute-start | bytes 786440 | tf_op jit(solution)/shard_map/ppermute | solution.py:308
  80.6 0.0 collective-permute-done.3.t0
  80.6 0.0 collective-permute-done.4.t1
  80.6 0.0 collective-permute-done.5.t2
  80.6 0.0 copy-done.1
  80.7 0.0 copy-done
  80.7 0.0 copy-done.4
  80.7 0.0 copy-done.5
  80.7 0.0 copy-start.2
  80.7 0.9 copy-done.2
  81.6 0.0 copy-start.3
  81.6 0.0 copy-start.6
  81.6 3.7 %shard_map.125 = bf16[32,512]{1,0:T(8,128)(2,1)S(1)} custom-call(bf16[1024,128]{1,0:T(8,128)(2,1)S(1)} %bitcast.21, s32[64,128]{1,0:T(8,128)S(1)} %copy-done.4, bf16[256,512]{1,0:T(8,128)(2,1)S(1)} %copy-done.2, f32[4,512]{1,0:T(4,128)S(1)} %copy-done.5, bf16[4,3,512,128]{3,2,1,0:T(8,128)(2,1)S(1)} %copy-done, bf16[4,3,128,512]{3,2,1,0:T(8,128)(2,1)S(1)} %copy-done.1, ...), custom_call_target="tpu_custom_call" | custom-call | flops 268435456 | bytes 8388608 | tf_op jit(solution)/shard_map/pallas_call | solution.py:240
  85.4 0.7 collective-permute-start.6
  86.7 0.0 collective-permute-done.7.far
  86.7 0.0 collective-permute-done.6.hidden
  86.7 0.0 copy-done.3
  86.7 0.0 copy-done.6
  86.7 4.5 %shard_map.126 = f32[16,128]{1,0:T(8,128)S(1)} custom-call(s32[1]{0:T(128)S(6)} %copy.14.pos, bf16[32,512]{1,0:T(8,128)(2,1)S(1)} %collective-permute-done.6.hidden, f32[4,512]{1,0:T(4,128)S(1)} %copy-done.5, bf16[4,3,512,128]{3,2,1,0:T(8,128)(2,1)S(1)} %copy-done, bf16[4,3,128,512]{3,2,1,0:T(8,128)(2,1)S(1)} %copy-done.1, ...), custom_call_target="tpu_custom_call" | custom-call | flops 268435456 | bytes 8388608 | tf_op jit(solution)/shard_map/pallas_call | solution.py:240
  91.2 11.8 %all_to_all.28 = f32[4,16,128]{2,1,0:T(8,128)S(1)} all-to-all(f32[4,16,128]{2,1,0:T(8,128)S(1)} %broadcast_in_dim.4), channel_id=1, replica_groups=mesh['dp'=128,'mp'=4] {'mp'}, dimensions={0} | all-to-all | bytes 65536 | tf_op jit(solution)/shard_map/all_to_all | solution.py:30
  103.0 0.5 slice.19
  103.6 0.6 slice_bitcast_fusion.1
  (2 shorter events, 0.0 us)
Async XLA Ops:
  2.4 11.6 %copy-start.7 = (s32[128,16]{1,0:T(8,128)S(1)}, s32[128,16]{1,0:T(8,128)}, u32[]{:S(2)}) copy-start(s32[128,16]{1,0:T(8,128)} %get-tuple-element.11) | copy-start | bytes 24580
  2.4 78.2 %copy-start.1 = (bf16[4,3,128,512]{3,2,1,0:T(8,128)(2,1)S(1)}, bf16[4,3,128,512]{3,2,1,0:T(8,128)(2,1)}, u32[]{:S(2)}) copy-start(bf16[4,3,128,512]{3,2,1,0:T(8,128)(2,1)} %conv_b.4) | copy-start | bytes 4718596
  5.4 75.3 %copy-start = (bf16[4,3,512,128]{3,2,1,0:T(8,128)(2,1)S(1)}, bf16[4,3,512,128]{3,2,1,0:T(8,128)(2,1)}, u32[]{:S(2)}) copy-start(bf16[4,3,512,128]{3,2,1,0:T(8,128)(2,1)} %conv_a.4) | copy-start | bytes 4718596
  5.4 75.3 %copy-start.4 = (s32[64,128]{1,0:T(8,128)S(1)}, s32[64,128]{1,0:T(8,128)}, u32[]{:S(2)}) copy-start(s32[64,128]{1,0:T(8,128)} %get-tuple-element.12.code) | copy-start | bytes 98308
  5.4 75.3 %copy-start.5 = (f32[4,512]{1,0:T(4,128)S(1)}, f32[4,512]{1,0:T(4,128)}, u32[]{:S(2)}) copy-start(f32[4,512]{1,0:T(4,128)} %gains.3) | copy-start | bytes 24580
  5.4 51.7 %collective-permute-start = (bf16[2,4,3,128,128]{4,3,2,1,0:T(8,128)(2,1)}, bf16[2,4,3,128,128]{4,3,2,1,0:T(8,128)(2,1)}, u32[]{:S(2)}, u32[]{:S(2)}) collective-permute-start(bf16[2,4,3,128,128]{4,3,2,1,0:T(8,128)(2,1)} %get-tuple-element.15), channel_id=1, source_target_pairs={{2,3},{0,1},{6,7},{4,5},{10,11},{8,9},{14,15},{12,13},{18,19},{16,... | collective-permute-start | bytes 2359304 | tf_op jit(solution)/shard_map/ppermute | solution.py:294
  9.9 49.4 %collective-permute-start.1 = (bf16[2,4,3,128,128]{4,3,2,1,0:T(8,128)(2,1)}, bf16[2,4,3,128,128]{4,3,2,1,0:T(8,128)(2,1)}, u32[]{:S(2)}, u32[]{:S(2)}) collective-permute-start(bf16[2,4,3,128,128]{4,3,2,1,0:T(8,128)(2,1)} %get-tuple-element.16), channel_id=1, source_target_pairs={{0,3},{2,1},{4,7},{6,5},{8,11},{10,9},{12,15},{14,13},{16,19},{18,... | collective-permute-start | bytes 2359304 | tf_op jit(solution)/shard_map/ppermute | solution.py:294
  12.4 49.1 %collective-permute-start.2 = (bf16[2,4,3,128,128]{4,3,2,1,0:T(8,128)(2,1)}, bf16[2,4,3,128,128]{4,3,2,1,0:T(8,128)(2,1)}, u32[]{:S(2)}, u32[]{:S(2)}) collective-permute-start(bf16[2,4,3,128,128]{4,3,2,1,0:T(8,128)(2,1)} %get-tuple-element.17), channel_id=1, source_target_pairs={{1,3},{3,1},{5,7},{7,5},{9,11},{11,9},{13,15},{15,13},{17,19},{19,... | collective-permute-start | bytes 2359304 | tf_op jit(solution)/shard_map/ppermute | solution.py:294
  50.3 28.7 %all-to-all-start.1 = ((bf16[128,8,128]{2,1,0:T(8,128)(2,1)}), bf16[128,8,128]{2,1,0:T(8,128)(2,1)S(1)}, u32[]{:S(2)}, u32[]{:S(2)}) async-start(bf16[128,8,128]{2,1,0:T(8,128)(2,1)} %bitcast.23), calls=%async_computation.1 | async-start | bytes 524288 | tf_op jit(solution)/shard_map/all_to_all | solution.py:30
  57.2 23.4 %collective-permute-start.3 = (bf16[2,4,3,128,128]{4,3,2,1,0:T(8,128)(2,1)}, bf16[2,4,3,128,128]{4,3,2,1,0:T(8,128)(2,1)}, u32[]{:S(2)}, u32[]{:S(2)}) collective-permute-start(bf16[2,4,3,128,128]{4,3,2,1,0:T(8,128)(2,1)} %collective-permute-done.m0), channel_id=1, source_target_pairs={{0,4},{4,0},{8,12},{12,8},{16,20},{20,16},{24,28},{28,24},{32,36},... | collective-permute-start | bytes 2359304 | tf_op jit(solution)/shard_map/ppermute | solution.py:296
  59.2 21.4 %collective-permute-start.4 = (bf16[2,4,3,128,128]{4,3,2,1,0:T(8,128)(2,1)}, bf16[2,4,3,128,128]{4,3,2,1,0:T(8,128)(2,1)}, u32[]{:S(2)}, u32[]{:S(2)}) collective-permute-start(bf16[2,4,3,128,128]{4,3,2,1,0:T(8,128)(2,1)} %collective-permute-done.1.m1), channel_id=1, source_target_pairs={{0,4},{4,0},{8,12},{12,8},{16,20},{20,16},{24,28},{28,24},{32,36},... | collective-permute-start | bytes 2359304 | tf_op jit(solution)/shard_map/ppermute | solution.py:296
  61.5 19.1 %collective-permute-start.5 = (bf16[2,4,3,128,128]{4,3,2,1,0:T(8,128)(2,1)}, bf16[2,4,3,128,128]{4,3,2,1,0:T(8,128)(2,1)}, u32[]{:S(2)}, u32[]{:S(2)}) collective-permute-start(bf16[2,4,3,128,128]{4,3,2,1,0:T(8,128)(2,1)} %collective-permute-done.2.m2), channel_id=1, source_target_pairs={{0,4},{4,0},{8,12},{12,8},{16,20},{20,16},{24,28},{28,24},{32,36},... | collective-permute-start | bytes 2359304 | tf_op jit(solution)/shard_map/ppermute | solution.py:296
  79.0 7.7 %collective-permute-start.7 = (bf16[1024,128]{1,0:T(8,128)(2,1)S(1)}, bf16[1024,128]{1,0:T(8,128)(2,1)S(1)}, u32[]{:S(2)}, u32[]{:S(2)}) collective-permute-start(bf16[1024,128]{1,0:T(8,128)(2,1)S(1)} %bitcast.20), channel_id=1, source_target_pairs={{0,1},{4,5},{8,9},{12,13},{16,17},{20,21},{24,25},{28,29},{32,33},... | collective-permute-start | bytes 786440 | tf_op jit(solution)/shard_map/ppermute | solution.py:308
  80.7 1.0 copy-start.2
  81.6 5.1 %copy-start.3 = (bf16[512,256]{1,0:T(8,128)(2,1)S(1)}, bf16[512,256]{1,0:T(8,128)(2,1)}, u32[]{:S(2)}) copy-start(bf16[512,256]{1,0:T(8,128)(2,1)} %w_out.1) | copy-start | bytes 786436
  81.6 5.1 %copy-start.6 = (s32[1,128]{1,0:T(1,128)S(1)}, s32[1,128]{1,0:T(1,128)}, u32[]{:S(2)}) copy-start(s32[1,128]{1,0:T(1,128)} %count.1) | copy-start | bytes 1540
  85.4 1.3 %collective-permute-start.6 = (bf16[32,512]{1,0:T(8,128)(2,1)S(1)}, bf16[32,512]{1,0:T(8,128)(2,1)S(1)}, u32[]{:S(2)}, u32[]{:S(2)}) collective-permute-start(bf16[32,512]{1,0:T(8,128)(2,1)S(1)} %shard_map.125), channel_id=1, source_target_pairs={{3,1},{7,5},{11,9},{15,13},{19,17},{23,21},{27,25},{31,29},{35,33}... | collective-permute-start | bytes 98312 | tf_op jit(solution)/shard_map/ppermute | solution.py:318

commit v4 on v3

--- a/solution.py
+++ b/solution.py
@@ -79,7 +79,7 @@
     first, second = iota(grid, 0), iota(grid, 1)
     slot = jnp.sum(jnp.where(same & (first < second), 1.0, 0.0), axis=0, keepdims=True)
     slot_down = jnp.sum(jnp.where(same & (second < first), 1.0, 0.0), axis=1, keepdims=True)
-    code[...] = jnp.broadcast_to(8.0 * down[:, :1] + slot_down, (WINDOW, 128)).astype(jnp.int32)
+    code[...] = jnp.broadcast_to(CAP * down[:, :1] + slot_down, (WINDOW, 128)).astype(jnp.int32)
     of_owner = along == iota(along.shape, 0).astype(F32)
     rows = row_v[...].astype(F32)
     lane = iota((128, 128), 1)
@@ -112,20 +112,9 @@
     wait_all(stores)
 
 
-def pick_kernel(asked, table, out):
-    count = out.shape[0]
-    spread = (iota((count, 128), 0) // 8 == iota((count, 128), 1)).astype(BF16)
-    wanted = asked[...]
-    high = dot(spread, (wanted // 64).astype(F32).astype(BF16))
-    low = dot(spread, (wanted % 64).astype(F32).astype(BF16))
-    here = iota(high.shape, 0) % 4 == iota(high.shape, 1)
-    ids = jnp.sum(jnp.where(here, 64.0 * high + low, 0.0), axis=1, keepdims=True).astype(jnp.int32)
-    rows = 256
-    for at in range(0, count, rows):
-        onehot = (ids[at : at + rows] == iota((rows, table.shape[0]), 1)).astype(F32).astype(BF16)
-        both = dot(onehot, table[...])
-        second = iota((rows, 128), 0) % 8 >= 4
-        out[at : at + rows, :] = jnp.where(second, both[:, 128:], both[:, :128]).astype(BF16)
+def pick_rows(table, ids):
+    onehot = (ids[:, None] == jnp.arange(table.shape[0], dtype=jnp.int32)[None, :]).astype(BF16)
+    return dot(onehot, table).astype(BF16)
 
 
 def block(hidden, j, gap, core_even, gain, conv_a, conv_b, mine, theirs):
@@ -163,70 +152,70 @@
     return ((summed - row_mean) * lax.rsqrt(row_var + 1e-05) * gain).astype(BF16)
 
 
-def weight_copies(conv_a, conv_b, moved, own_a, own_b, mine, theirs, sems):
-    base = jnp.where(lax.axis_index("mp") == SECOND, 2, 0)
+def weight_copies(moved, mine, theirs, sems):
     copies = []
     for j in range(2):
-        pairs = [(conv_a.at[base + j], own_a.at[j]), (conv_b.at[base + j], own_b.at[j])]
-        pairs += [(moved[i].at[j], mine.at[i, j]) for i in range(3)]
+        pairs = [(moved[i].at[j], mine.at[i, j]) for i in range(3)]
         pairs += [(moved[3 + i].at[j], theirs.at[i, j]) for i in range(3)]
-        copies.append([pltpu.make_async_copy(a, b, sems.at[8 * j + n]) for n, (a, b) in enumerate(pairs)])
+        copies.append([pltpu.make_async_copy(a, b, sems.at[6 * j + n]) for n, (a, b) in enumerate(pairs)])
     return copies
 
 
-WEIGHT_SCRATCH = (
-    pltpu.VMEM((2, 3, C, QUARTER), BF16),
-    pltpu.VMEM((2, 3, QUARTER, C), BF16),
-    pltpu.VMEM((3,) + WEIGHTS, BF16),
-    pltpu.VMEM((3,) + WEIGHTS, BF16),
-    pltpu.SemaphoreType.DMA((16,)),
+KEPT = (
+    jax.ShapeDtypeStruct((3,) + WEIGHTS, BF16),
+    jax.ShapeDtypeStruct((3,) + WEIGHTS, BF16),
 )
 
 
-def two_blocks(hidden, stage, gains, copies, own_a, own_b, mine, theirs):
+def two_blocks(hidden, stage, gains, own_a, own_b, mine, theirs, ready):
     core_even = core_of() == 0
     for j, gap in ((0, 1), (1, 4)):
-        wait_all(copies[j])
+        ready(j)
         gain = gains[pl.ds(2 * stage + j, 1), :]
         hidden = block(hidden, j, gap, core_even, gain, own_a, own_b, mine, theirs)
     return hidden
 
 
-def first_kernel(arrived, code, w_in, gains, conv_a, conv_b, m0, m1, m2, t0, t1, t2, out, own_a, own_b, mine, theirs, sems):
-    copies = weight_copies(conv_a, conv_b, (m0, m1, m2, t0, t1, t2), own_a, own_b, mine, theirs, sems)
+def first_kernel(arrived, code, w_in, gains, own_a, own_b, m0, m1, m2, t0, t1, t2, out, mine, theirs, sems):
+    copies = weight_copies((m0, m1, m2, t0, t1, t2), mine, theirs, sems)
     start_all(copies[0])
     start_all(copies[1])
-    at = code[:, :1]
-    lanes = iota((WINDOW, arrived.shape[0]), 1)
-    picked = [dot((at + 4 * half == lanes).astype(F32).astype(BF16), arrived[...]) for half in range(2)]
-    embedded = jnp.concatenate(picked, axis=1).astype(BF16)
-    hidden = dot(embedded, w_in[...]).astype(BF16)
-    out[...] = two_blocks(hidden, 0, gains, copies, own_a, own_b, mine, theirs)[LATE:]
-
-
-def second_kernel(
-    pos, hidden, gains, conv_a, conv_b, m0, m1, m2, t0, t1, t2, w_out, near, far, count, out, own_a, own_b, mine, theirs, sems
-):
-    copies = weight_copies(conv_a, conv_b, (m0, m1, m2, t0, t1, t2), own_a, own_b, mine, theirs, sems)
-    start_all(copies[0])
-    start_all(copies[1])
-    last = two_blocks(hidden[...], 1, gains, copies, own_a, own_b, mine, theirs)
-    vec = dot(last[LATE - 16 :], w_out[...]).astype(BF16)
+    is_first = lax.axis_index("mp") == FIRST
+
+    @pl.when(is_first)
+    def _():
+        onehot = (code[:, :1] == iota((WINDOW, arrived.shape[0]), 1)).astype(F32).astype(BF16)
+        hidden = dot(dot(onehot, arrived[...]).astype(BF16), w_in[...]).astype(BF16)
+        ready = lambda j: wait_all(copies[j])
+        out[...] = two_blocks(hidden, 0, gains, own_a, own_b, mine, theirs, ready)[LATE:]
+
+    @pl.when(jnp.logical_not(is_first))
+    def _():
+        wait_all(copies[0])
+        wait_all(copies[1])
+
+
+def second_kernel(pos, hidden, gains, own_a, own_b, mine, theirs, w_out, near, far, count, out):
+    @pl.when(lax.axis_index("mp") == SECOND)
+    def _():
+        last = two_blocks(hidden[...], 1, gains, own_a, own_b, mine, theirs, lambda j: None)
+        score(dot(last[LATE - 16 :], w_out[...]).astype(BF16), pos, near, far, count, out)
+
+
+def score(vec, pos, near, far, count, out):
     grid = (CPO, near.shape[0])
-    second = iota((1, near.shape[0]), 1) % 8 >= 4
 
     def scored(rows):
-        halves = [dot_t(vec[:, at : at + 128], rows[...])[15:16] for at in (0, 128)]
-        return jnp.broadcast_to(0.25 * jnp.where(second, halves[1], halves[0]), grid)
+        return jnp.broadcast_to(0.25 * dot_t(vec, rows[...])[15:16], grid)
 
     slot, lane = iota(grid, 0), iota(grid, 1)
-    kept = jnp.where(lane % 4 == slot % 4, jnp.where(slot < CAP, scored(near), scored(far)), 0.0)
+    kept = jnp.where(lane % CAP == slot % CAP, jnp.where(slot < CAP, scored(near), scored(far)), 0.0)
     pieces, rest = [], kept
     for _ in range(3):
         piece = rest.astype(BF16)
         pieces.append(piece.astype(F32))
         rest = rest - piece.astype(F32)
-    owners = (iota((grid[1], 128), 0) // 8 == iota((grid[1], 128), 1)).astype(F32).astype(BF16)
+    owners = (iota((grid[1], 128), 0) // CAP == iota((grid[1], 128), 1)).astype(F32).astype(BF16)
     sums = dot(jnp.concatenate(pieces, axis=0).astype(BF16), owners)
     raw = sums[:CPO] + sums[CPO : 2 * CPO] + sums[2 * CPO :]
     valid = iota(raw.shape, 0) < count[...]
@@ -295,35 +284,30 @@
     for half in moved[:3]:
         moved.append(lax.ppermute(half, "dp", [(i, i ^ 1) for i in range(dp_count)]))
 
-    picked = call(
-        pick_kernel,
-        jax.ShapeDtypeStruct((dp_count * 8, 128), BF16),
-        (asked, item_table),
-        (VMEM, VMEM),
+    picked = pick_rows(item_table, asked[:, :CAP].reshape(-1)).reshape(dp_count, CAP, -1)
+    arrived = exchange(picked, "dp").reshape(dp_count * CAP, -1)
+    base = jnp.where(lax.axis_index("mp") == SECOND, 2, 0)
+    own_a = lax.dynamic_slice_in_dim(pack_a, base, 2)
+    own_b = lax.dynamic_slice_in_dim(pack_b, base, 2)
+    far = lax.ppermute(arrived, "mp", [(0, SECOND)])
+    hidden, *kept = call(
+        first_kernel,
+        (jax.ShapeDtypeStruct((LATE, C), BF16),) + KEPT,
+        (arrived, code, w_in, gains, own_a, own_b, *moved),
+        (VMEM,) * 6 + (HBM,) * 6,
         VMEM,
-        [],
-        60,
-    )
-    arrived = exchange(picked, "dp")
-    far = lax.ppermute(arrived, "mp", [(0, SECOND)])
-    hidden = call(
-        first_kernel,
-        jax.ShapeDtypeStruct((LATE, C), BF16),
-        (arrived, code, w_in, gains, conv_a, conv_b, *moved),
-        (VMEM,) * 4 + (HBM,) * 8,
-        VMEM,
-        WEIGHT_SCRATCH,
-        24,
+        [pltpu.SemaphoreType.DMA((12,))],
+        16,
     )
     hidden = lax.ppermute(hidden, "mp", [(FIRST, SECOND)])
     packed_out = call(
         second_kernel,
         jax.ShapeDtypeStruct((2 * CPO, dp_count), F32),
-        (pos_owner, hidden, gains, conv_a, conv_b, *moved, w_out, arrived, far, cand_count),
-        (SMEM, VMEM, VMEM) + (HBM,) * 8 + (VMEM,) * 4,
+        (pos_owner, hidden, gains, own_a, own_b, *kept, w_out, arrived, far, cand_count),
+        (SMEM,) + (VMEM,) * 10,
         VMEM,
-        WEIGHT_SCRATCH,
-        24,
+        [],
+        8,
     )
     shared = exchange(jnp.broadcast_to(packed_out[None], (mp_count,) + packed_out.shape), "mp")[SECOND]
     return (shared[:CPO].T[None], shared[CPO, :1])

time: 105 us -> 97 us (0.924)
  blocking collectives: 44.6 us -> 13.9 us
  starting transfers between devices: 24.1 us -> 49.2 us
  Pallas kernels: 16.4 us -> 7.19 us
  waiting for transfers between devices: 15.4 us -> 18.5 us
  local copies, waits for them, and re-layouts: 2.09 us -> 4.49 us
    all_to_all x2 -> x1, blocking collectives: 44.6 us -> 13.9 us  [exchange(): return lax.all_to_all(values, axis, split_axis=0, concat_axis=0, tiled=True)]
    all_to_all x1 -> x2, starting transfers between devices: 6.86 us -> 32.2 us  [exchange(): return lax.all_to_all(values, axis, split_axis=0, concat_axis=0, tiled=True)]
    ppermute x3, waiting for transfers between devices: 0.01 us -> 12.7 us  [forward(): lax.ppermute(half, 'mp', [(to_first, FIRST), (to_second, SECOND)])]
    all_to_all x1 -> x2, waiting for transfers between devices: 15.4 us -> 5.81 us  [exchange(): return lax.all_to_all(values, axis, split_axis=0, concat_axis=0, tiled=True)]
    pallas_call x5 -> x4, Pallas kernels: 16.4 us -> 7.19 us  [call(): pl.pallas_call(kernel, out_shape=out_shape, in_specs=[pl.BlockSpec(memory...]
    dynamic_slice x0 -> x2, local copies, waits for them, and re-layouts: none -> 2.4 us  [the longest x1 1.21 us: forward(): own_b = lax.dynamic_slice_in_dim(pack_b, base, 2)]
  transfers between devices with their start and end apart: 9 -> 10, of which waited for: 1 -> 3; matrix products, arithmetic and copies ran while one was open for 0% -> 4% of each run, Pallas kernels for 7% -> 6%
where the time goes in v4:
time: 97 us; the launch traced here: 95.8 us
  starting transfers between devices  49.2 us (51%)
  waiting for transfers between devices  18.5 us (19%)
  blocking collectives  13.9 us (14%)
  Pallas kernels  7.19 us (7%)
  local copies, waits for them, and re-layouts  4.49 us (5%)
  between operations  1.57 us (2%)
    all_to_all x2, starting transfers between devices, exchange(): return lax.all_to_all(values, axis, split_axis=0, concat_axis=0, tiled=True)  32.2 us
    all_to_all x1, blocking collectives, exchange(): return lax.all_to_all(values, axis, split_axis=0, concat_axis=0, tiled=True)  13.9 us
    ppermute x3, waiting for transfers between devices, forward(): lax.ppermute(half, 'mp', [(to_first, FIRST), (to_second, SECOND)])  12.7 us
    ppermute x3, starting transfers between devices, forward(): lax.ppermute(half, 'mp', [(to_first, FIRST), (to_second, SECOND)])  7.56 us
    pallas_call x4, Pallas kernels, call(): pl.pallas_call(kernel, out_shape=out_shape, in_specs=[pl.BlockSpec(memory...  7.19 us
    ppermute x3, starting transfers between devices, forward(): lax.ppermute(half, 'dp', [(i, i ^ 1) for i in range(dp_count)])  6.34 us
    all_to_all x2, waiting for transfers between devices, exchange(): return lax.all_to_all(values, axis, split_axis=0, concat_axis=0, tiled=True)  5.81 us
    ppermute x1, starting transfers between devices, forward(): far = lax.ppermute(arrived, 'mp', [(0, SECOND)])  2.49 us
  transfers between devices with their start and end apart: 10, of which 3 were waited for; matrix products, arithmetic and copies ran while one was open for 4% of the time, Pallas kernels for 6%

profile of v4, /device:TPU:24, one launch (start us, length us, event | category | flops | bytes accessed | tf_op | source)
XLA Modules:
  0.0 95.8 jit_solution(16158961156019587328)
XLA Ops:
  0.6 0.0 copy-start
  0.6 1.9 %shard_map.122 = (s32[128,16]{1,0:T(8,128)}, s32[64,128]{1,0:T(8,128)}) custom-call(s32[1,64]{1,0:T(1,128)} %bitcast.23, s32[1,64]{1,0:T(1,128)} %bitcast.24, s32[8,128]{1,0:T(8,128)} %bitcast.22), custom_call_target="tpu_custom_call" | custom-call | flops 268435456 | bytes 8388608 | tf_op jit(solution)/shard_map/pallas_call | solution.py:229
  2.5 19.3 %all-to-all-start = ((s32[128,1,16]{2,1,0:T(1,128)}), s32[128,1,16]{2,1,0:T(1,128)S(1)}, u32[]{:S(2)}, u32[]{:S(2)}) async-start(s32[128,1,16]{2,1,0:T(1,128)} %bitcast.21), calls=%async_computation | async-start | bytes 131072 | tf_op jit(solution)/shard_map/all_to_all | solution.py:30
  21.8 2.9 %shard_map.123 = (bf16[2,4,3,128,128]{4,3,2,1,0:T(8,128)(2,1)}, bf16[2,4,3,128,128]{4,3,2,1,0:T(8,128)(2,1)}, bf16[2,4,3,128,128]{4,3,2,1,0:T(8,128)(2,1)}) custom-call(bf16[4,3,512,128]{3,2,1,0:T(8,128)(2,1)} %conv_a, bf16[4,3,128,512]{3,2,1,0:T(8,128)(2,1)} %conv_b), custom_call_target="tpu_custom_call" | custom-call | flops 268435456 | bytes 8388608 | tf_op jit(solution)/shard_map/pallas_call | solution.py:229
  24.7 3.4 %collective-permute-start = (bf16[2,4,3,128,128]{4,3,2,1,0:T(8,128)(2,1)}, bf16[2,4,3,128,128]{4,3,2,1,0:T(8,128)(2,1)S(1)}, u32[]{:S(2)}, u32[]{:S(2)}) collective-permute-start(bf16[2,4,3,128,128]{4,3,2,1,0:T(8,128)(2,1)} %get-tuple-element.18), channel_id=1, source_target_pairs={{2,3},{0,1},{6,7},{4,5},{10,11},{8,9},{14,15},{12,13},{18,19},{16,... | collective-permute-start | bytes 2359304 | tf_op jit(solution)/shard_map/ppermute | solution.py:283
  28.2 2.6 %collective-permute-start.1 = (bf16[2,4,3,128,128]{4,3,2,1,0:T(8,128)(2,1)}, bf16[2,4,3,128,128]{4,3,2,1,0:T(8,128)(2,1)S(1)}, u32[]{:S(2)}, u32[]{:S(2)}) collective-permute-start(bf16[2,4,3,128,128]{4,3,2,1,0:T(8,128)(2,1)} %get-tuple-element.19), channel_id=1, source_target_pairs={{0,3},{2,1},{4,7},{6,5},{8,11},{10,9},{12,15},{14,13},{16,19},{18,... | collective-permute-start | bytes 2359304 | tf_op jit(solution)/shard_map/ppermute | solution.py:283
  30.8 1.6 %collective-permute-start.2 = (bf16[2,4,3,128,128]{4,3,2,1,0:T(8,128)(2,1)}, bf16[2,4,3,128,128]{4,3,2,1,0:T(8,128)(2,1)}, u32[]{:S(2)}, u32[]{:S(2)}) collective-permute-start(bf16[2,4,3,128,128]{4,3,2,1,0:T(8,128)(2,1)} %get-tuple-element.20), channel_id=1, source_target_pairs={{1,3},{3,1},{5,7},{7,5},{9,11},{11,9},{13,15},{15,13},{17,19},{19,... | collective-permute-start | bytes 2359304 | tf_op jit(solution)/shard_map/ppermute | solution.py:283
  32.3 3.2 %all-to-all-done = s32[128,1,16]{2,1,0:T(1,128)S(1)} async-done(((s32[128,1,16]{2,1,0:T(1,128)}), s32[128,1,16]{2,1,0:T(1,128)S(1)}, u32[]{:S(2)}, u32[]{:S(2)}) %all-to-all-start) | async-done | bytes 8224 | tf_op jit(solution)/shard_map/all_to_all | solution.py:30
  35.5 0.1 eq.18
  35.6 0.0 copy-done
  35.7 0.9 fusion.2
  36.5 0.0 copy-start.1
  36.5 0.0 copy-start.3
  36.5 0.0 copy-start.4
  36.6 0.8 reshape.23
  37.3 12.9 %all-to-all-start.1 = ((bf16[128,4,256]{2,1,0:T(4,128)(2,1)}), bf16[128,4,256]{2,1,0:T(4,128)(2,1)S(1)}, u32[]{:S(2)}, u32[]{:S(2)}) async-start(bf16[128,4,256]{2,1,0:T(4,128)(2,1)} %reshape.23), calls=%async_computation.1 | async-start | bytes 524288 | tf_op jit(solution)/shard_map/all_to_all | solution.py:30
  50.2 0.0 collective-permute-done.m0
  50.2 2.0 %collective-permute-start.3 = (bf16[2,4,3,128,128]{4,3,2,1,0:T(8,128)(2,1)S(1)}, bf16[2,4,3,128,128]{4,3,2,1,0:T(8,128)(2,1)}, u32[]{:S(2)}, u32[]{:S(2)}) collective-permute-start(bf16[2,4,3,128,128]{4,3,2,1,0:T(8,128)(2,1)S(1)} %collective-permute-done.m0), channel_id=1, source_target_pairs={{0,4},{4,0},{8,12},{12,8},{16,20},{20,16},{24,28},{28,24},{32,36},... | collective-permute-start | bytes 2359304 | tf_op jit(solution)/shard_map/ppermute | solution.py:285
  52.3 12.7 %collective-permute-done.1.m1 = bf16[2,4,3,128,128]{4,3,2,1,0:T(8,128)(2,1)S(1)} collective-permute-done((bf16[2,4,3,128,128]{4,3,2,1,0:T(8,128)(2,1)}, bf16[2,4,3,128,128]{4,3,2,1,0:T(8,128)(2,1)S(1)}, u32[]{:S(2)}, u32[]{:S(2)}) %collective-permute-start.1) | collective-permute-done | bytes 786464 | tf_op jit(solution)/shard_map/ppermute | solution.py:283
  64.9 1.9 %collective-permute-start.4 = (bf16[2,4,3,128,128]{4,3,2,1,0:T(8,128)(2,1)S(1)}, bf16[2,4,3,128,128]{4,3,2,1,0:T(8,128)(2,1)}, u32[]{:S(2)}, u32[]{:S(2)}) collective-permute-start(bf16[2,4,3,128,128]{4,3,2,1,0:T(8,128)(2,1)S(1)} %collective-permute-done.1.m1), channel_id=1, source_target_pairs={{0,4},{4,0},{8,12},{12,8},{16,20},{20,16},{24,28},{28,24},{32,36},... | collective-permute-start | bytes 2359304 | tf_op jit(solution)/shard_map/ppermute | solution.py:285
  66.9 0.0 collective-permute-done.2.m2
  66.9 2.4 %collective-permute-start.5 = (bf16[2,4,3,128,128]{4,3,2,1,0:T(8,128)(2,1)}, bf16[2,4,3,128,128]{4,3,2,1,0:T(8,128)(2,1)}, u32[]{:S(2)}, u32[]{:S(2)}) collective-permute-start(bf16[2,4,3,128,128]{4,3,2,1,0:T(8,128)(2,1)} %collective-permute-done.2.m2), channel_id=1, source_target_pairs={{0,4},{4,0},{8,12},{12,8},{16,20},{20,16},{24,28},{28,24},{32,36},... | collective-permute-start | bytes 2359304 | tf_op jit(solution)/shard_map/ppermute | solution.py:285
  69.3 2.6 %all-to-all-done.1 = bf16[128,4,256]{2,1,0:T(4,128)(2,1)S(1)} async-done(((bf16[128,4,256]{2,1,0:T(4,128)(2,1)}), bf16[128,4,256]{2,1,0:T(4,128)(2,1)S(1)}, u32[]{:S(2)}, u32[]{:S(2)}) %all-to-all-start.1) | async-done | bytes 262176 | tf_op jit(solution)/shard_map/all_to_all | solution.py:30
  71.9 0.1 reshape.24.arrived.near
  71.9 2.5 %collective-permute-start.7 = (bf16[512,256]{1,0:T(8,128)(2,1)S(1)}, bf16[512,256]{1,0:T(8,128)(2,1)S(1)}, u32[]{:S(2)}, u32[]{:S(2)}) collective-permute-start(bf16[512,256]{1,0:T(8,128)(2,1)S(1)} %reshape.24.arrived.near), channel_id=1, source_target_pairs={{0,1},{4,5},{8,9},{12,13},{16,17},{20,21},{24,25},{28,29},{32,33},... | collective-permute-start | bytes 786440 | tf_op jit(solution)/shard_map/ppermute | solution.py:292
  74.4 1.2 %constant_dynamic-slice_fusion.own_b = bf16[2,3,128,512]{3,2,1,0:T(8,128)(2,1)S(1)} fusion(bf16[4,3,128,512]{3,2,1,0:T(8,128)(2,1)} %conv_b, s32[]{:T(128)S(6)} %select_n.6), kind=kLoop, calls=%fused_computation.6 | loop fusion | bytes 1572868 | tf_op jit(solution)/shard_map/dynamic_slice | solution.py:291
  75.7 1.2 %constant_dynamic-slice_fusion.1.own_a = bf16[2,3,512,128]{3,2,1,0:T(8,128)(2,1)S(1)} fusion(bf16[4,3,512,128]{3,2,1,0:T(8,128)(2,1)} %conv_a, s32[]{:T(128)S(6)} %select_n.6), kind=kLoop, calls=%fused_computation.7 | loop fusion | bytes 1572868 | tf_op jit(solution)/shard_map/dynamic_slice | solution.py:290
  76.9 0.0 collective-permute-done.3.t0
  76.9 0.0 collective-permute-done.4.t1
  76.9 0.0 collective-permute-done.5.t2
  76.9 0.0 copy-done.1
  76.9 0.0 copy-done.3
  76.9 0.0 copy-done.4
  76.9 0.0 copy-start.2
  76.9 0.0 copy-start.5
  76.9 2.4 %shard_map.124 = (bf16[32,512]{1,0:T(8,128)(2,1)S(1)}, bf16[3,2,4,3,128,128]{5,4,3,2,1,0:T(8,128)(2,1)S(1)}, bf16[3,2,4,3,128,128]{5,4,3,2,1,0:T(8,128)(2,1)S(1)}) custom-call(bf16[512,256]{1,0:T(8,128)(2,1)S(1)} %reshape.24.arrived.near, s32[64,128]{1,0:T(8,128)S(1)} %copy-done.3, bf16[256,512]{1,0:T(8,128)(2,1)S(1)} %copy-done.1, f32[4,512]{1,0:T(4,128)S(1)} %copy-done.4, ...), custom_call_target="tpu_custom_call" | custom-call | flops 268435456 | bytes 8388608 | tf_op jit(solution)/shard_map/pallas_call | solution.py:229
  79.4 0.7 collective-permute-start.6
  80.7 0.0 collective-permute-done.7.far
  80.7 0.0 collective-permute-done.6.hidden
  80.7 0.0 copy-done.2
  80.7 0.0 copy-done.5
  80.7 13.9 %all_to_all.22 = f32[4,16,128]{2,1,0:T(8,128)S(1)} all-to-all(f32[4,16,128]{2,1,0:T(8,128)S(1)} %broadcast_in_dim.4), channel_id=1, replica_groups=mesh['dp'=128,'mp'=4] {'mp'}, dimensions={0} | all-to-all | bytes 65536 | tf_op jit(solution)/shard_map/all_to_all | solution.py:30
  94.7 0.5 slice.24
  95.2 0.6 slice_bitcast_fusion.1
  (3 shorter events, 0.0 us)
Async XLA Ops:
  0.6 35.0 %copy-start = (bf16[2048,256]{1,0:T(8,128)(2,1)S(1)}, bf16[2048,256]{1,0:T(8,128)(2,1)}, u32[]{:S(2)}) copy-start(bf16[2048,256]{1,0:T(8,128)(2,1)} %param.11) | copy-start | bytes 3145732
  2.5 33.0 %all-to-all-start = ((s32[128,1,16]{2,1,0:T(1,128)}), s32[128,1,16]{2,1,0:T(1,128)S(1)}, u32[]{:S(2)}, u32[]{:S(2)}) async-start(s32[128,1,16]{2,1,0:T(1,128)} %bitcast.21), calls=%async_computation | async-start | bytes 131072 | tf_op jit(solution)/shard_map/all_to_all | solution.py:30
  24.7 25.5 %collective-permute-start = (bf16[2,4,3,128,128]{4,3,2,1,0:T(8,128)(2,1)}, bf16[2,4,3,128,128]{4,3,2,1,0:T(8,128)(2,1)S(1)}, u32[]{:S(2)}, u32[]{:S(2)}) collective-permute-start(bf16[2,4,3,128,128]{4,3,2,1,0:T(8,128)(2,1)} %get-tuple-element.18), channel_id=1, source_target_pairs={{2,3},{0,1},{6,7},{4,5},{10,11},{8,9},{14,15},{12,13},{18,19},{16,... | collective-permute-start | bytes 2359304 | tf_op jit(solution)/shard_map/ppermute | solution.py:283
  28.2 36.7 %collective-permute-start.1 = (bf16[2,4,3,128,128]{4,3,2,1,0:T(8,128)(2,1)}, bf16[2,4,3,128,128]{4,3,2,1,0:T(8,128)(2,1)S(1)}, u32[]{:S(2)}, u32[]{:S(2)}) collective-permute-start(bf16[2,4,3,128,128]{4,3,2,1,0:T(8,128)(2,1)} %get-tuple-element.19), channel_id=1, source_target_pairs={{0,3},{2,1},{4,7},{6,5},{8,11},{10,9},{12,15},{14,13},{16,19},{18,... | collective-permute-start | bytes 2359304 | tf_op jit(solution)/shard_map/ppermute | solution.py:283
  30.8 36.1 %collective-permute-start.2 = (bf16[2,4,3,128,128]{4,3,2,1,0:T(8,128)(2,1)}, bf16[2,4,3,128,128]{4,3,2,1,0:T(8,128)(2,1)}, u32[]{:S(2)}, u32[]{:S(2)}) collective-permute-start(bf16[2,4,3,128,128]{4,3,2,1,0:T(8,128)(2,1)} %get-tuple-element.20), channel_id=1, source_target_pairs={{1,3},{3,1},{5,7},{7,5},{9,11},{11,9},{13,15},{15,13},{17,19},{19,... | collective-permute-start | bytes 2359304 | tf_op jit(solution)/shard_map/ppermute | solution.py:283
  36.5 40.4 %copy-start.1 = (bf16[256,512]{1,0:T(8,128)(2,1)S(1)}, bf16[256,512]{1,0:T(8,128)(2,1)}, u32[]{:S(2)}) copy-start(bf16[256,512]{1,0:T(8,128)(2,1)} %w_in.1) | copy-start | bytes 786436
  36.5 40.4 %copy-start.3 = (s32[64,128]{1,0:T(8,128)S(1)}, s32[64,128]{1,0:T(8,128)}, u32[]{:S(2)}) copy-start(s32[64,128]{1,0:T(8,128)} %get-tuple-element.15.code) | copy-start | bytes 98308
  36.5 40.4 %copy-start.4 = (f32[4,512]{1,0:T(4,128)S(1)}, f32[4,512]{1,0:T(4,128)}, u32[]{:S(2)}) copy-start(f32[4,512]{1,0:T(4,128)} %gains.3) | copy-start | bytes 24580
  37.3 34.5 %all-to-all-start.1 = ((bf16[128,4,256]{2,1,0:T(4,128)(2,1)}), bf16[128,4,256]{2,1,0:T(4,128)(2,1)S(1)}, u32[]{:S(2)}, u32[]{:S(2)}) async-start(bf16[128,4,256]{2,1,0:T(4,128)(2,1)} %reshape.23), calls=%async_computation.1 | async-start | bytes 524288 | tf_op jit(solution)/shard_map/all_to_all | solution.py:30
  50.2 26.6 %collective-permute-start.3 = (bf16[2,4,3,128,128]{4,3,2,1,0:T(8,128)(2,1)S(1)}, bf16[2,4,3,128,128]{4,3,2,1,0:T(8,128)(2,1)}, u32[]{:S(2)}, u32[]{:S(2)}) collective-permute-start(bf16[2,4,3,128,128]{4,3,2,1,0:T(8,128)(2,1)S(1)} %collective-permute-done.m0), channel_id=1, source_target_pairs={{0,4},{4,0},{8,12},{12,8},{16,20},{20,16},{24,28},{28,24},{32,36},... | collective-permute-start | bytes 2359304 | tf_op jit(solution)/shard_map/ppermute | solution.py:285
  64.9 11.9 %collective-permute-start.4 = (bf16[2,4,3,128,128]{4,3,2,1,0:T(8,128)(2,1)S(1)}, bf16[2,4,3,128,128]{4,3,2,1,0:T(8,128)(2,1)}, u32[]{:S(2)}, u32[]{:S(2)}) collective-permute-start(bf16[2,4,3,128,128]{4,3,2,1,0:T(8,128)(2,1)S(1)} %collective-permute-done.1.m1), channel_id=1, source_target_pairs={{0,4},{4,0},{8,12},{12,8},{16,20},{20,16},{24,28},{28,24},{32,36},... | collective-permute-start | bytes 2359304 | tf_op jit(solution)/shard_map/ppermute | solution.py:285
  66.9 10.0 %collective-permute-start.5 = (bf16[2,4,3,128,128]{4,3,2,1,0:T(8,128)(2,1)}, bf16[2,4,3,128,128]{4,3,2,1,0:T(8,128)(2,1)}, u32[]{:S(2)}, u32[]{:S(2)}) collective-permute-start(bf16[2,4,3,128,128]{4,3,2,1,0:T(8,128)(2,1)} %collective-permute-done.2.m2), channel_id=1, source_target_pairs={{0,4},{4,0},{8,12},{12,8},{16,20},{20,16},{24,28},{28,24},{32,36},... | collective-permute-start | bytes 2359304 | tf_op jit(solution)/shard_map/ppermute | solution.py:285
  71.9 8.7 %collective-permute-start.7 = (bf16[512,256]{1,0:T(8,128)(2,1)S(1)}, bf16[512,256]{1,0:T(8,128)(2,1)S(1)}, u32[]{:S(2)}, u32[]{:S(2)}) collective-permute-start(bf16[512,256]{1,0:T(8,128)(2,1)S(1)} %reshape.24.arrived.near), channel_id=1, source_target_pairs={{0,1},{4,5},{8,9},{12,13},{16,17},{20,21},{24,25},{28,29},{32,33},... | collective-permute-start | bytes 786440 | tf_op jit(solution)/shard_map/ppermute | solution.py:292
  76.9 3.8 %copy-start.2 = (bf16[512,256]{1,0:T(8,128)(2,1)S(1)}, bf16[512,256]{1,0:T(8,128)(2,1)}, u32[]{:S(2)}) copy-start(bf16[512,256]{1,0:T(8,128)(2,1)} %w_out.1) | copy-start | bytes 786436
  76.9 3.8 %copy-start.5 = (s32[1,128]{1,0:T(1,128)S(1)}, s32[1,128]{1,0:T(1,128)}, u32[]{:S(2)}) copy-start(s32[1,128]{1,0:T(1,128)} %count.1) | copy-start | bytes 1540
  79.4 1.3 %collective-permute-start.6 = (bf16[32,512]{1,0:T(8,128)(2,1)S(1)}, bf16[32,512]{1,0:T(8,128)(2,1)S(1)}, u32[]{:S(2)}, u32[]{:S(2)}) collective-permute-start(bf16[32,512]{1,0:T(8,128)(2,1)S(1)} %get-tuple-element.21), channel_id=1, source_target_pairs={{3,1},{7,5},{11,9},{15,13},{19,17},{23,21},{27,25},{31,29},{35,33}... | collective-permute-start | bytes 98312 | tf_op jit(solution)/shard_map/ppermute | solution.py:302

commit v5 on v4

--- a/solution.py
+++ b/solution.py
@@ -94,7 +94,7 @@
     out[...] = jnp.where(mp_index == FIRST, history, cands).astype(jnp.int32)[:, : out.shape[1]]
 
 
-def pack_kernel(conv_a, conv_b, out_0, out_1, out_2, packed, sems):
+def pack_kernel(conv_a, conv_b, out_0, out_1, out_2, out_3, packed, sems):
     side = pl.multiple_of(core_of() * 256, 256)
     mp_index = lax.axis_index("mp")
     loads = []
@@ -105,9 +105,10 @@
     start_all(loads)
     wait_all(loads)
     stores = []
-    for i, ((to_first, _), out) in enumerate(zip(WEIGHT_MOVES, (out_0, out_1, out_2))):
-        start = jnp.where(mp_index == to_first, 0, 2)
-        stores.append(pltpu.make_async_copy(packed.at[pl.ds(start, 2)], out, sems.at[4 + i]))
+    outs = ((out_0, 0, 0, 2), (out_1, 1, 0, 2), (out_2, 2, 0, 1), (out_3, 2, 1, 1))
+    for i, (out, move, skip, blocks) in enumerate(outs):
+        start = jnp.where(mp_index == WEIGHT_MOVES[move][0], 0, 2) + skip
+        stores.append(pltpu.make_async_copy(packed.at[pl.ds(start, blocks)], out, sems.at[4 + i]))
     start_all(stores)
     wait_all(stores)
 
@@ -155,8 +156,9 @@
 def weight_copies(moved, mine, theirs, sems):
     copies = []
     for j in range(2):
-        pairs = [(moved[i].at[j], mine.at[i, j]) for i in range(3)]
-        pairs += [(moved[3 + i].at[j], theirs.at[i, j]) for i in range(3)]
+        pairs = []
+        for into, (whole_0, whole_1, *blocks) in ((mine, moved[:4]), (theirs, moved[4:])):
+            pairs += [(whole_0.at[j], into.at[0, j]), (whole_1.at[j], into.at[1, j]), (blocks[j].at[0], into.at[2, j])]
         copies.append([pltpu.make_async_copy(a, b, sems.at[6 * j + n]) for n, (a, b) in enumerate(pairs)])
     return copies
 
@@ -176,8 +178,9 @@
     return hidden
 
 
-def first_kernel(arrived, code, w_in, gains, own_a, own_b, m0, m1, m2, t0, t1, t2, out, mine, theirs, sems):
-    copies = weight_copies((m0, m1, m2, t0, t1, t2), mine, theirs, sems)
+def first_kernel(arrived, code, w_in, gains, own_a, own_b, *refs):
+    *moved, out, mine, theirs, sems = refs
+    copies = weight_copies(moved, mine, theirs, sems)
     start_all(copies[0])
     start_all(copies[1])
     is_first = lax.axis_index("mp") == FIRST
@@ -271,30 +274,33 @@
 
     sent = call(
         pack_kernel,
-        [jax.ShapeDtypeStruct(WEIGHTS, BF16)] * 3,
+        [jax.ShapeDtypeStruct(WEIGHTS, BF16)] * 2 + [jax.ShapeDtypeStruct((1,) + WEIGHTS[1:], BF16)] * 2,
         (pack_a, pack_b),
         (HBM, HBM),
         HBM,
-        [pltpu.VMEM((BLOCKS, 4, 3, 128, 128), BF16), pltpu.SemaphoreType.DMA((7,))],
+        [pltpu.VMEM((BLOCKS, 4, 3, 128, 128), BF16), pltpu.SemaphoreType.DMA((8,))],
         60,
     )
     moved = []
     for (to_first, to_second), half in zip(WEIGHT_MOVES, sent):
         moved.append(lax.ppermute(half, "mp", [(to_first, FIRST), (to_second, SECOND)]))
-    for half in moved[:3]:
-        moved.append(lax.ppermute(half, "dp", [(i, i ^ 1) for i in range(dp_count)]))
-
-    picked = pick_rows(item_table, asked[:, :CAP].reshape(-1)).reshape(dp_count, CAP, -1)
-    arrived = exchange(picked, "dp").reshape(dp_count * CAP, -1)
+    halfway = lax.ppermute(sent[3], "mp", [(1, 2), (3, 0)])
+    moved.append(lax.ppermute(halfway, "mp", [(2, FIRST), (0, SECOND)]))
     base = jnp.where(lax.axis_index("mp") == SECOND, 2, 0)
     own_a = lax.dynamic_slice_in_dim(pack_a, base, 2)
     own_b = lax.dynamic_slice_in_dim(pack_b, base, 2)
+    first_swap, own_a, own_b = lax.optimization_barrier((moved[0], own_a, own_b))
+    for half in [first_swap] + moved[1:]:
+        moved.append(lax.ppermute(half, "dp", [(i, i ^ 1) for i in range(dp_count)]))
+
+    picked = pick_rows(item_table, asked[:, :CAP].reshape(-1)).reshape(dp_count, CAP, -1)
+    arrived = exchange(picked, "dp").reshape(dp_count * CAP, -1)
     far = lax.ppermute(arrived, "mp", [(0, SECOND)])
     hidden, *kept = call(
         first_kernel,
         (jax.ShapeDtypeStruct((LATE, C), BF16),) + KEPT,
         (arrived, code, w_in, gains, own_a, own_b, *moved),
-        (VMEM,) * 6 + (HBM,) * 6,
+        (VMEM,) * 6 + (HBM,) * 8,
         VMEM,
         [pltpu.SemaphoreType.DMA((12,))],
         16,

time: 97 us -> 107 us (1.10)
  blocking collectives: 13.9 us -> 45.1 us
  starting transfers between devices: 49.2 us -> 32.1 us
  waiting for transfers between devices: 18.5 us -> 13.2 us
  local copies, waits for them, and re-layouts: 4.49 us -> 6.18 us
    all_to_all x1 -> x2, blocking collectives: 13.9 us -> 45.1 us  [exchange(): return lax.all_to_all(values, axis, split_axis=0, concat_axis=0, tiled=True)]
    all_to_all x2 -> x1, starting transfers between devices: 32.2 us -> 7.95 us  [exchange(): return lax.all_to_all(values, axis, split_axis=0, concat_axis=0, tiled=True)]
    ppermute x3, waiting for transfers between devices: 12.7 us -> 0.01 us  [forward(): lax.ppermute(half, 'mp', [(to_first, FIRST), (to_second, SECOND)])]
    ppermute x0 -> x2, waiting for transfers between devices: none -> 11.5 us  [the longest x1 10.2 us: forward(): halfway = lax.ppermute(sent[3], 'mp', [(1, 2), (3, 0)])]
    all_to_all x2 -> x1, waiting for transfers between devices: 5.81 us -> 0.01 us  [exchange(): return lax.all_to_all(values, axis, split_axis=0, concat_axis=0, tiled=True)]
    ppermute x0 -> x2, starting transfers between devices: none -> 3.33 us  [the longest x1 2.04 us: forward(): moved.append(lax.ppermute(halfway, 'mp', [(2, FIRST), (0, SECOND)]))]
    ppermute x1, starting transfers between devices: 2.49 us -> 4.4 us  [forward(): far = lax.ppermute(arrived, 'mp', [(0, SECOND)])]
    ppermute x3 -> x4, starting transfers between devices: 6.34 us -> 8.15 us  [forward(): lax.ppermute(half, 'dp', [(i, i ^ 1) for i in range(dp_count)])]
  transfers between devices with their start and end apart: 10 -> 12, of which waited for: 3 -> 3; matrix products, arithmetic and copies ran while one was open for 4% -> 5% of each run, Pallas kernels for 6% -> 2%
where the time goes in v5:
time: 107 us; the launch traced here: 106 us
  blocking collectives  45.1 us (42%)
  starting transfers between devices  32.1 us (30%)
  waiting for transfers between devices  13.2 us (12%)
  Pallas kernels  7.14 us (7%)
  local copies, waits for them, and re-layouts  6.18 us (6%)
  between operations  1.54 us (1%)
    all_to_all x2, blocking collectives, exchange(): return lax.all_to_all(values, axis, split_axis=0, concat_axis=0, tiled=True)  45.1 us
    ppermute x1, waiting for transfers between devices, forward(): halfway = lax.ppermute(sent[3], 'mp', [(1, 2), (3, 0)])  10.2 us
    ppermute x4, starting transfers between devices, forward(): lax.ppermute(half, 'dp', [(i, i ^ 1) for i in range(dp_count)])  8.15 us
    all_to_all x1, starting transfers between devices, exchange(): return lax.all_to_all(values, axis, split_axis=0, concat_axis=0, tiled=True)  7.95 us
    ppermute x3, starting transfers between devices, forward(): lax.ppermute(half, 'mp', [(to_first, FIRST), (to_second, SECOND)])  7.57 us
    pallas_call x4, Pallas kernels, call(): pl.pallas_call(kernel, out_shape=out_shape, in_specs=[pl.BlockSpec(memory...  7.14 us
    ppermute x1, starting transfers between devices, forward(): far = lax.ppermute(arrived, 'mp', [(0, SECOND)])  4.4 us
  transfers between devices with their start and end apart: 12, of which 3 were waited for; matrix products, arithmetic and copies ran while one was open for 5% of the time, Pallas kernels for 2%

profile of v5, /device:TPU:24, one launch (start us, length us, event | category | flops | bytes accessed | tf_op | source)
XLA Modules:
  0.0 106.1 jit_solution(9504262252491237120)
XLA Ops:
  0.6 0.0 copy-start
  0.6 1.9 %shard_map.122 = (s32[128,16]{1,0:T(8,128)}, s32[64,128]{1,0:T(8,128)}) custom-call(s32[1,64]{1,0:T(1,128)} %bitcast.23, s32[1,64]{1,0:T(1,128)} %bitcast.24, s32[8,128]{1,0:T(8,128)} %bitcast.22), custom_call_target="tpu_custom_call" | custom-call | flops 268435456 | bytes 8388608 | tf_op jit(solution)/shard_map/pallas_call | solution.py:232
  2.5 0.0 copy-start.6
  2.5 2.9 %shard_map.123 = (bf16[2,4,3,128,128]{4,3,2,1,0:T(8,128)(2,1)}, bf16[2,4,3,128,128]{4,3,2,1,0:T(8,128)(2,1)}, bf16[1,4,3,128,128]{4,3,2,1,0:T(8,128)(2,1)}, bf16[1,4,3,128,128]{4,3,2,1,0:T(8,128)(2,1)}) custom-call(bf16[4,3,512,128]{3,2,1,0:T(8,128)(2,1)} %conv_a, bf16[4,3,128,512]{3,2,1,0:T(8,128)(2,1)} %conv_b), custom_call_target="tpu_custom_call" | custom-call | flops 268435456 | bytes 8388608 | tf_op jit(solution)/shard_map/pallas_call | solution.py:232
  5.4 4.3 %collective-permute-start = (bf16[2,4,3,128,128]{4,3,2,1,0:T(8,128)(2,1)}, bf16[2,4,3,128,128]{4,3,2,1,0:T(8,128)(2,1)}, u32[]{:S(2)}, u32[]{:S(2)}) collective-permute-start(bf16[2,4,3,128,128]{4,3,2,1,0:T(8,128)(2,1)} %get-tuple-element.22), channel_id=1, source_target_pairs={{2,3},{0,1},{6,7},{4,5},{10,11},{8,9},{14,15},{12,13},{18,19},{16,... | collective-permute-start | bytes 2359304 | tf_op jit(solution)/shard_map/ppermute | solution.py:286
  9.7 2.6 %collective-permute-start.1 = (bf16[2,4,3,128,128]{4,3,2,1,0:T(8,128)(2,1)}, bf16[2,4,3,128,128]{4,3,2,1,0:T(8,128)(2,1)}, u32[]{:S(2)}, u32[]{:S(2)}) collective-permute-start(bf16[2,4,3,128,128]{4,3,2,1,0:T(8,128)(2,1)} %get-tuple-element.25), channel_id=1, source_target_pairs={{0,3},{2,1},{4,7},{6,5},{8,11},{10,9},{12,15},{14,13},{16,19},{18,... | collective-permute-start | bytes 2359304 | tf_op jit(solution)/shard_map/ppermute | solution.py:286
  12.3 0.0 copy-done.6
  12.3 32.8 %all_to_all.22 = s32[128,1,16]{2,1,0:T(1,128)S(1)} all-to-all(s32[128,1,16]{2,1,0:T(1,128)S(1)} %bitcast.21), channel_id=1, replica_groups=mesh['dp'=128,'mp'=4] {'dp'}, dimensions={0} | all-to-all | bytes 16384 | tf_op jit(solution)/shard_map/all_to_all | solution.py:30
  45.1 0.1 eq.18
  45.2 0.0 copy-done
  45.3 0.9 fusion.2
  46.1 0.0 copy-start.1
  46.1 0.0 copy-start.4
  46.2 0.8 reshape.23
  46.9 7.9 %all-to-all-start.1 = ((bf16[128,4,256]{2,1,0:T(4,128)(2,1)}), bf16[128,4,256]{2,1,0:T(4,128)(2,1)}, u32[]{:S(2)}, u32[]{:S(2)}) async-start(bf16[128,4,256]{2,1,0:T(4,128)(2,1)} %reshape.23), calls=%async_computation.1 | async-start | bytes 524288 | tf_op jit(solution)/shard_map/all_to_all | solution.py:30
  54.9 1.3 %collective-permute-start.3 = (bf16[1,4,3,128,128]{4,3,2,1,0:T(8,128)(2,1)}, bf16[1,4,3,128,128]{4,3,2,1,0:T(8,128)(2,1)}, u32[]{:S(2)}, u32[]{:S(2)}) collective-permute-start(bf16[1,4,3,128,128]{4,3,2,1,0:T(8,128)(2,1)} %get-tuple-element.27), channel_id=1, source_target_pairs={{1,2},{3,0},{5,6},{7,4},{9,10},{11,8},{13,14},{15,12},{17,18},{19,... | collective-permute-start | bytes 1179656 | tf_op jit(solution)/shard_map/ppermute | solution.py:287
  56.2 0.7 collective-permute-start.2
  56.9 1.2 %constant_dynamic-slice_fusion.own_b = bf16[2,3,128,512]{3,2,1,0:T(8,128)(2,1)S(1)} fusion(bf16[4,3,128,512]{3,2,1,0:T(8,128)(2,1)} %conv_b, s32[]{:T(128)S(6)} %select_n.6), kind=kLoop, calls=%fused_computation.6 | loop fusion | bytes 1572868 | tf_op jit(solution)/shard_map/dynamic_slice | solution.py:291
  58.1 1.2 %constant_dynamic-slice_fusion.1.own_a = bf16[2,3,512,128]{3,2,1,0:T(8,128)(2,1)S(1)} fusion(bf16[4,3,512,128]{3,2,1,0:T(8,128)(2,1)} %conv_a, s32[]{:T(128)S(6)} %select_n.6), kind=kLoop, calls=%fused_computation.7 | loop fusion | bytes 1572868 | tf_op jit(solution)/shard_map/dynamic_slice | solution.py:290
  59.3 10.2 %collective-permute-done.3 = bf16[1,4,3,128,128]{4,3,2,1,0:T(8,128)(2,1)} collective-permute-done((bf16[1,4,3,128,128]{4,3,2,1,0:T(8,128)(2,1)}, bf16[1,4,3,128,128]{4,3,2,1,0:T(8,128)(2,1)}, u32[]{:S(2)}, u32[]{:S(2)}) %collective-permute-start.3) | collective-permute-done | bytes 393248 | tf_op jit(solution)/shard_map/ppermute | solution.py:287
  69.5 2.0 %collective-permute-start.4 = (bf16[1,4,3,128,128]{4,3,2,1,0:T(8,128)(2,1)}, bf16[1,4,3,128,128]{4,3,2,1,0:T(8,128)(2,1)}, u32[]{:S(2)}, u32[]{:S(2)}) collective-permute-start(bf16[1,4,3,128,128]{4,3,2,1,0:T(8,128)(2,1)} %collective-permute-done.3), channel_id=1, source_target_pairs={{2,3},{0,1},{6,7},{4,5},{10,11},{8,9},{14,15},{12,13},{18,19},{16,... | collective-permute-start | bytes 1179656 | tf_op jit(solution)/shard_map/ppermute | solution.py:288
  71.5 0.0 collective-permute-done.refs_0_
  71.5 1.9 %collective-permute-start.5 = (bf16[2,4,3,128,128]{4,3,2,1,0:T(8,128)(2,1)}, bf16[2,4,3,128,128]{4,3,2,1,0:T(8,128)(2,1)}, u32[]{:S(2)}, u32[]{:S(2)}) collective-permute-start(bf16[2,4,3,128,128]{4,3,2,1,0:T(8,128)(2,1)} %collective-permute-done.refs_0_), channel_id=1, source_target_pairs={{0,4},{4,0},{8,12},{12,8},{16,20},{20,16},{24,28},{28,24},{32,36},... | collective-permute-start | bytes 2359304 | tf_op jit(solution)/shard_map/ppermute | solution.py:294
  73.4 0.0 collective-permute-done.1.refs_1_
  73.4 2.4 %collective-permute-start.6 = (bf16[2,4,3,128,128]{4,3,2,1,0:T(8,128)(2,1)}, bf16[2,4,3,128,128]{4,3,2,1,0:T(8,128)(2,1)}, u32[]{:S(2)}, u32[]{:S(2)}) collective-permute-start(bf16[2,4,3,128,128]{4,3,2,1,0:T(8,128)(2,1)} %collective-permute-done.1.refs_1_), channel_id=1, source_target_pairs={{0,4},{4,0},{8,12},{12,8},{16,20},{20,16},{24,28},{28,24},{32,36},... | collective-permute-start | bytes 2359304 | tf_op jit(solution)/shard_map/ppermute | solution.py:294
  75.8 0.0 collective-permute-done.2.refs_2_
  75.9 1.9 %collective-permute-start.7 = (bf16[1,4,3,128,128]{4,3,2,1,0:T(8,128)(2,1)S(1)}, bf16[1,4,3,128,128]{4,3,2,1,0:T(8,128)(2,1)}, u32[]{:S(2)}, u32[]{:S(2)}) collective-permute-start(bf16[1,4,3,128,128]{4,3,2,1,0:T(8,128)(2,1)S(1)} %collective-permute-done.2.refs_2_), channel_id=1, source_target_pairs={{0,4},{4,0},{8,12},{12,8},{16,20},{20,16},{24,28},{28,24},{32,36},... | collective-permute-start | bytes 1179656 | tf_op jit(solution)/shard_map/ppermute | solution.py:294
  77.8 1.3 %collective-permute-done.4.refs_3_ = bf16[1,4,3,128,128]{4,3,2,1,0:T(8,128)(2,1)} collective-permute-done((bf16[1,4,3,128,128]{4,3,2,1,0:T(8,128)(2,1)}, bf16[1,4,3,128,128]{4,3,2,1,0:T(8,128)(2,1)}, u32[]{:S(2)}, u32[]{:S(2)}) %collective-permute-start.4) | collective-permute-done | bytes 393248 | tf_op jit(solution)/shard_map/ppermute | solution.py:288
  79.1 1.9 %collective-permute-start.8 = (bf16[1,4,3,128,128]{4,3,2,1,0:T(8,128)(2,1)}, bf16[1,4,3,128,128]{4,3,2,1,0:T(8,128)(2,1)}, u32[]{:S(2)}, u32[]{:S(2)}) collective-permute-start(bf16[1,4,3,128,128]{4,3,2,1,0:T(8,128)(2,1)} %collective-permute-done.4.refs_3_), channel_id=1, source_target_pairs={{0,4},{4,0},{8,12},{12,8},{16,20},{20,16},{24,28},{28,24},{32,36},... | collective-permute-start | bytes 1179656 | tf_op jit(solution)/shard_map/ppermute | solution.py:294
  81.0 0.0 all-to-all-done.1
  81.1 1.0 reshape.24.arrived.near
  82.1 4.4 %collective-permute-start.10 = (bf16[512,256]{1,0:T(8,128)(2,1)S(1)}, bf16[512,256]{1,0:T(8,128)(2,1)S(1)}, u32[]{:S(2)}, u32[]{:S(2)}) collective-permute-start(bf16[512,256]{1,0:T(8,128)(2,1)S(1)} %reshape.24.arrived.near), channel_id=1, source_target_pairs={{0,1},{4,5},{8,9},{12,13},{16,17},{20,21},{24,25},{28,29},{32,33},... | collective-permute-start | bytes 786440 | tf_op jit(solution)/shard_map/ppermute | solution.py:298
  86.5 0.0 collective-permute-done.7.refs_6_
  86.5 0.0 collective-permute-done.8.refs_7_
  86.5 0.0 collective-permute-done.5.refs_4_
  86.5 0.0 collective-permute-done.6.refs_5_
  86.5 0.0 copy-done.1
  86.5 0.0 copy-done.4
  86.5 0.0 copy-start.3
  86.6 0.7 copy-done.3
  87.3 0.0 copy-start.2
  87.3 0.0 copy-start.5
  87.3 2.4 %shard_map.124 = (bf16[32,512]{1,0:T(8,128)(2,1)S(1)}, bf16[3,2,4,3,128,128]{5,4,3,2,1,0:T(8,128)(2,1)S(1)}, bf16[3,2,4,3,128,128]{5,4,3,2,1,0:T(8,128)(2,1)S(1)}) custom-call(bf16[512,256]{1,0:T(8,128)(2,1)S(1)} %reshape.24.arrived.near, s32[64,128]{1,0:T(8,128)S(1)} %copy-done.3, bf16[256,512]{1,0:T(8,128)(2,1)S(1)} %copy-done.1, f32[4,512]{1,0:T(4,128)S(1)} %copy-done.4, ...), custom_call_target="tpu_custom_call" | custom-call | flops 268435456 | bytes 8388608 | tf_op jit(solution)/shard_map/pallas_call | solution.py:232
  89.7 0.7 collective-permute-start.9
  91.0 1.7 %collective-permute-done.10.far = bf16[512,256]{1,0:T(8,128)(2,1)S(1)} collective-permute-done((bf16[512,256]{1,0:T(8,128)(2,1)S(1)}, bf16[512,256]{1,0:T(8,128)(2,1)S(1)}, u32[]{:S(2)}, u32[]{:S(2)}) %collective-permute-start.10) | collective-permute-done | bytes 262176 | tf_op jit(solution)/shard_map/ppermute | solution.py:298
  92.7 0.0 collective-permute-done.9.hidden
  92.7 0.0 copy-done.2
  92.7 0.0 copy-done.5
  92.7 12.2 %all_to_all.23 = f32[4,16,128]{2,1,0:T(8,128)S(1)} all-to-all(f32[4,16,128]{2,1,0:T(8,128)S(1)} %broadcast_in_dim.4), channel_id=1, replica_groups=mesh['dp'=128,'mp'=4] {'mp'}, dimensions={0} | all-to-all | bytes 65536 | tf_op jit(solution)/shard_map/all_to_all | solution.py:30
  105.0 0.5 slice.24
  105.5 0.6 slice_bitcast_fusion.1
  (3 shorter events, 0.0 us)
Async XLA Ops:
  0.6 44.6 %copy-start = (bf16[2048,256]{1,0:T(8,128)(2,1)S(1)}, bf16[2048,256]{1,0:T(8,128)(2,1)}, u32[]{:S(2)}) copy-start(bf16[2048,256]{1,0:T(8,128)(2,1)} %param.11) | copy-start | bytes 3145732
  2.5 9.8 %copy-start.6 = (s32[128,16]{1,0:T(8,128)S(1)}, s32[128,16]{1,0:T(8,128)}, u32[]{:S(2)}) copy-start(s32[128,16]{1,0:T(8,128)} %get-tuple-element.18) | copy-start | bytes 24580
  5.4 66.1 %collective-permute-start = (bf16[2,4,3,128,128]{4,3,2,1,0:T(8,128)(2,1)}, bf16[2,4,3,128,128]{4,3,2,1,0:T(8,128)(2,1)}, u32[]{:S(2)}, u32[]{:S(2)}) collective-permute-start(bf16[2,4,3,128,128]{4,3,2,1,0:T(8,128)(2,1)} %get-tuple-element.22), channel_id=1, source_target_pairs={{2,3},{0,1},{6,7},{4,5},{10,11},{8,9},{14,15},{12,13},{18,19},{16,... | collective-permute-start | bytes 2359304 | tf_op jit(solution)/shard_map/ppermute | solution.py:286
  9.7 63.7 %collective-permute-start.1 = (bf16[2,4,3,128,128]{4,3,2,1,0:T(8,128)(2,1)}, bf16[2,4,3,128,128]{4,3,2,1,0:T(8,128)(2,1)}, u32[]{:S(2)}, u32[]{:S(2)}) collective-permute-start(bf16[2,4,3,128,128]{4,3,2,1,0:T(8,128)(2,1)} %get-tuple-element.25), channel_id=1, source_target_pairs={{0,3},{2,1},{4,7},{6,5},{8,11},{10,9},{12,15},{14,13},{16,19},{18,... | collective-permute-start | bytes 2359304 | tf_op jit(solution)/shard_map/ppermute | solution.py:286
  46.1 40.4 %copy-start.1 = (bf16[256,512]{1,0:T(8,128)(2,1)S(1)}, bf16[256,512]{1,0:T(8,128)(2,1)}, u32[]{:S(2)}) copy-start(bf16[256,512]{1,0:T(8,128)(2,1)} %w_in.1) | copy-start | bytes 786436
  46.1 40.4 %copy-start.4 = (f32[4,512]{1,0:T(4,128)S(1)}, f32[4,512]{1,0:T(4,128)}, u32[]{:S(2)}) copy-start(f32[4,512]{1,0:T(4,128)} %gains.3) | copy-start | bytes 24580
  46.9 34.1 %all-to-all-start.1 = ((bf16[128,4,256]{2,1,0:T(4,128)(2,1)}), bf16[128,4,256]{2,1,0:T(4,128)(2,1)}, u32[]{:S(2)}, u32[]{:S(2)}) async-start(bf16[128,4,256]{2,1,0:T(4,128)(2,1)} %reshape.23), calls=%async_computation.1 | async-start | bytes 524288 | tf_op jit(solution)/shard_map/all_to_all | solution.py:30
  54.9 14.6 %collective-permute-start.3 = (bf16[1,4,3,128,128]{4,3,2,1,0:T(8,128)(2,1)}, bf16[1,4,3,128,128]{4,3,2,1,0:T(8,128)(2,1)}, u32[]{:S(2)}, u32[]{:S(2)}) collective-permute-start(bf16[1,4,3,128,128]{4,3,2,1,0:T(8,128)(2,1)} %get-tuple-element.27), channel_id=1, source_target_pairs={{1,2},{3,0},{5,6},{7,4},{9,10},{11,8},{13,14},{15,12},{17,18},{19,... | collective-permute-start | bytes 1179656 | tf_op jit(solution)/shard_map/ppermute | solution.py:287
  56.2 19.7 %collective-permute-start.2 = (bf16[1,4,3,128,128]{4,3,2,1,0:T(8,128)(2,1)}, bf16[1,4,3,128,128]{4,3,2,1,0:T(8,128)(2,1)S(1)}, u32[]{:S(2)}, u32[]{:S(2)}) collective-permute-start(bf16[1,4,3,128,128]{4,3,2,1,0:T(8,128)(2,1)} %get-tuple-element.26), channel_id=1, source_target_pairs={{1,3},{3,1},{5,7},{7,5},{9,11},{11,9},{13,15},{15,13},{17,19},{19,... | collective-permute-start | bytes 1179656 | tf_op jit(solution)/shard_map/ppermute | solution.py:286
  69.5 9.7 %collective-permute-start.4 = (bf16[1,4,3,128,128]{4,3,2,1,0:T(8,128)(2,1)}, bf16[1,4,3,128,128]{4,3,2,1,0:T(8,128)(2,1)}, u32[]{:S(2)}, u32[]{:S(2)}) collective-permute-start(bf16[1,4,3,128,128]{4,3,2,1,0:T(8,128)(2,1)} %collective-permute-done.3), channel_id=1, source_target_pairs={{2,3},{0,1},{6,7},{4,5},{10,11},{8,9},{14,15},{12,13},{18,19},{16,... | collective-permute-start | bytes 1179656 | tf_op jit(solution)/shard_map/ppermute | solution.py:288
  71.5 15.0 %collective-permute-start.5 = (bf16[2,4,3,128,128]{4,3,2,1,0:T(8,128)(2,1)}, bf16[2,4,3,128,128]{4,3,2,1,0:T(8,128)(2,1)}, u32[]{:S(2)}, u32[]{:S(2)}) collective-permute-start(bf16[2,4,3,128,128]{4,3,2,1,0:T(8,128)(2,1)} %collective-permute-done.refs_0_), channel_id=1, source_target_pairs={{0,4},{4,0},{8,12},{12,8},{16,20},{20,16},{24,28},{28,24},{32,36},... | collective-permute-start | bytes 2359304 | tf_op jit(solution)/shard_map/ppermute | solution.py:294
  73.4 13.1 %collective-permute-start.6 = (bf16[2,4,3,128,128]{4,3,2,1,0:T(8,128)(2,1)}, bf16[2,4,3,128,128]{4,3,2,1,0:T(8,128)(2,1)}, u32[]{:S(2)}, u32[]{:S(2)}) collective-permute-start(bf16[2,4,3,128,128]{4,3,2,1,0:T(8,128)(2,1)} %collective-permute-done.1.refs_1_), channel_id=1, source_target_pairs={{0,4},{4,0},{8,12},{12,8},{16,20},{20,16},{24,28},{28,24},{32,36},... | collective-permute-start | bytes 2359304 | tf_op jit(solution)/shard_map/ppermute | solution.py:294
  75.9 10.6 %collective-permute-start.7 = (bf16[1,4,3,128,128]{4,3,2,1,0:T(8,128)(2,1)S(1)}, bf16[1,4,3,128,128]{4,3,2,1,0:T(8,128)(2,1)}, u32[]{:S(2)}, u32[]{:S(2)}) collective-permute-start(bf16[1,4,3,128,128]{4,3,2,1,0:T(8,128)(2,1)S(1)} %collective-permute-done.2.refs_2_), channel_id=1, source_target_pairs={{0,4},{4,0},{8,12},{12,8},{16,20},{20,16},{24,28},{28,24},{32,36},... | collective-permute-start | bytes 1179656 | tf_op jit(solution)/shard_map/ppermute | solution.py:294
  79.1 7.4 %collective-permute-start.8 = (bf16[1,4,3,128,128]{4,3,2,1,0:T(8,128)(2,1)}, bf16[1,4,3,128,128]{4,3,2,1,0:T(8,128)(2,1)}, u32[]{:S(2)}, u32[]{:S(2)}) collective-permute-start(bf16[1,4,3,128,128]{4,3,2,1,0:T(8,128)(2,1)} %collective-permute-done.4.refs_3_), channel_id=1, source_target_pairs={{0,4},{4,0},{8,12},{12,8},{16,20},{20,16},{24,28},{28,24},{32,36},... | collective-permute-start | bytes 1179656 | tf_op jit(solution)/shard_map/ppermute | solution.py:294
  82.1 10.6 %collective-permute-start.10 = (bf16[512,256]{1,0:T(8,128)(2,1)S(1)}, bf16[512,256]{1,0:T(8,128)(2,1)S(1)}, u32[]{:S(2)}, u32[]{:S(2)}) collective-permute-start(bf16[512,256]{1,0:T(8,128)(2,1)S(1)} %reshape.24.arrived.near), channel_id=1, source_target_pairs={{0,1},{4,5},{8,9},{12,13},{16,17},{20,21},{24,25},{28,29},{32,33},... | collective-permute-start | bytes 786440 | tf_op jit(solution)/shard_map/ppermute | solution.py:298
  86.5 0.8 copy-start.3
  87.3 5.4 %copy-start.2 = (bf16[512,256]{1,0:T(8,128)(2,1)S(1)}, bf16[512,256]{1,0:T(8,128)(2,1)}, u32[]{:S(2)}) copy-start(bf16[512,256]{1,0:T(8,128)(2,1)} %w_out.1) | copy-start | bytes 786436
  87.3 5.4 %copy-start.5 = (s32[1,128]{1,0:T(1,128)S(1)}, s32[1,128]{1,0:T(1,128)}, u32[]{:S(2)}) copy-start(s32[1,128]{1,0:T(1,128)} %count.1) | copy-start | bytes 1540
  89.7 3.0 %collective-permute-start.9 = (bf16[32,512]{1,0:T(8,128)(2,1)S(1)}, bf16[32,512]{1,0:T(8,128)(2,1)S(1)}, u32[]{:S(2)}, u32[]{:S(2)}) collective-permute-start(bf16[32,512]{1,0:T(8,128)(2,1)S(1)} %get-tuple-element.29), channel_id=1, source_target_pairs={{3,1},{7,5},{11,9},{15,13},{19,17},{23,21},{27,25},{31,29},{35,33}... | collective-permute-start | bytes 98312 | tf_op jit(solution)/shard_map/ppermute | solution.py:308
